TPU v7x, 512 devices: a whole 4x8x8 slice. The times are simulated.
512 devices in a mesh: replica: 16 (over x, y_hi), shard: 32 (over y_lo, z, core).
Axes of the slice: x: 4, y: 8 (y_hi: 4, y_lo: 2; y = y_hi * 2 + y_lo), z: 8, core: 2. Of those that a mesh axis runs over, the one named last changes fastest.
Arguments:
- inputs: bfloat16 [131072, 6144], P(('replica', 'shard')), may hold values from -6 to 6
- doc_ids: int32 [512, 256], P(('replica', 'shard')), may hold values from 0 to 7, never falling along the last dimension, each value on 1 to 64 neighbouring positions
- values: bfloat16 [131072, 128], P(('replica', 'shard')), may hold values from -6 to 6
- cotangent: bfloat16 [131072, 128], P(('replica', 'shard')), may hold values from -24 to 24
- weights: float32 [98304, 256], P(('replica', 'shard')), may hold values from -6 to 6
- moment1: float32 [98304, 256], P(('replica', 'shard')), may hold values from -3 to 3
- moment2: float32 [98304, 256], P(('replica', 'shard')), may hold values from 0.05 to 2
- frag_local: bfloat16 [16, 16, 32, 6144], P('replica', None, 'shard'), may hold values from -6 to 6
- frag_global: float32 [16, 32, 6144], P(None, 'shard'), may hold values from -6 to 6
- frag_moment: float32 [16, 32, 6144], P(None, 'shard'), may hold values from -3 to 3
- frag_index: int32 [1], replicated, may hold values from 0 to 15
Outputs:
- new_weights: float32 [98304, 256], P(('replica', 'shard'))
- new_moment1: float32 [98304, 256], P(('replica', 'shard'))
- new_moment2: float32 [98304, 256], P(('replica', 'shard'))
- new_global: float32 [32, 6144], P('shard')
- new_moment: float32 [32, 6144], P('shard')
Inputs may be any that keep to these rules, and one draw needn't show every extreme that they name: `doc_ids`: within each row document numbers start at 0, never fall, and each document has 1 to 64 tokens; some document has exactly 64.
All inputs are finite; a program needn't handle non-finite values.
Results may differ from a plain program's by a relative error of at most 0.008.
Values may be sent and summed in bfloat16 or wider, within the bound.
A program may use at most 64 MiB of HBM per device.

v0:
```python
import math

import jax
import jax.numpy as jnp
from jax import lax
from jax.sharding import PartitionSpec as P

ADAM_STEP = 100


epsilon = 1e-06
beta_one = 0.9
beta_two = 0.95
learn_rate = 0.01
decay_rate = 0.1
outer_momentum = 0.9
outer_rate = 0.7


def head_grads(inputs, doc_ids, values, cotangent, projected):
    model_width = inputs.shape[1]
    head_size = values.shape[1]
    input_scale = 1.0 / math.sqrt(model_width)
    score_scale = 1.0 / math.sqrt(head_size)
    scaled = projected * input_scale
    queries = scaled[:, :head_size]
    keys_part = scaled[:, head_size:]
    q_rate = lax.rsqrt(jnp.mean(queries * queries, axis=1, keepdims=True) + epsilon)
    k_rate = lax.rsqrt(jnp.mean(keys_part * keys_part, axis=1, keepdims=True) + epsilon)
    q_unit = queries * q_rate
    k_unit = keys_part * k_rate
    scores = jnp.dot(q_unit, k_unit.T, precision=lax.Precision.HIGHEST) * score_scale
    position = jnp.arange(doc_ids.shape[0])
    allowed = (doc_ids[:, None] == doc_ids[None, :]) & (position[None, :] <= position[:, None])
    raised = jnp.where(allowed, jnp.exp(scores), jnp.float32(0.0))
    attention = raised / jnp.sum(raised, axis=1, keepdims=True)
    grad_attention = jnp.dot(cotangent, values.T, preferred_element_type=jnp.float32)
    grad_scores = (
        attention
        * (grad_attention - jnp.sum(attention * grad_attention, axis=1, keepdims=True))
        * score_scale
    )
    grad_qunit = jnp.dot(grad_scores, k_unit, precision=lax.Precision.HIGHEST)
    grad_kunit = jnp.dot(grad_scores.T, q_unit, precision=lax.Precision.HIGHEST)
    grad_query = q_rate * (
        grad_qunit - q_unit * jnp.mean(grad_qunit * q_unit, axis=1, keepdims=True)
    )
    grad_keys = k_rate * (
        grad_kunit - k_unit * jnp.mean(grad_kunit * k_unit, axis=1, keepdims=True)
    )
    return (jnp.concatenate([grad_query, grad_keys], axis=1) * input_scale).astype(jnp.bfloat16)


def inner_step(inputs, doc_ids, values, cotangent, weights, moment1, moment2):
    lowered = weights.astype(jnp.bfloat16)
    gathered = lax.all_gather(lowered, "shard", axis=0, tiled=True)
    projected = jnp.dot(inputs, gathered, preferred_element_type=jnp.float32)
    grad_projected = head_grads(inputs, doc_ids[0], values, cotangent, projected)
    grad_term = lax.dot_general(
        inputs, grad_projected, (((0,), (0,)), ((), ())), preferred_element_type=jnp.float32
    )
    gradient = lax.psum_scatter(
        grad_term.astype(jnp.bfloat16), "shard", scatter_dimension=0, tiled=True
    ).astype(jnp.float32)
    first_new = beta_one * moment1 + (1.0 - beta_one) * gradient
    second_new = beta_two * moment2 + (1.0 - beta_two) * gradient * gradient
    first_hat = first_new / (1.0 - beta_one**ADAM_STEP)
    second_hat = second_new / (1.0 - beta_two**ADAM_STEP)
    weight_new = weights - learn_rate * (
        first_hat / (jnp.sqrt(second_hat) + 1e-08) + decay_rate * weights
    )
    return (weight_new, first_new, second_new)


def outer_step(frag_local, frag_global, frag_moment, frag_index):
    chosen = frag_index[0]
    current = lax.dynamic_index_in_dim(frag_global, chosen, 0, keepdims=False)
    moment_now = lax.dynamic_index_in_dim(frag_moment, chosen, 0, keepdims=False)
    local_copy = lax.dynamic_index_in_dim(frag_local[0], chosen, 0, keepdims=False)
    lowered_drift = lax.optimization_barrier(
        (current - local_copy.astype(jnp.float32)).astype(jnp.bfloat16)
    )
    drift = lowered_drift.astype(jnp.float32)
    replicas = lax.axis_size("replica")
    drift_mean = lax.psum(drift, "replica") / replicas
    new_moment = outer_momentum * moment_now + drift_mean
    new_global = current - outer_rate * (drift_mean + outer_momentum * new_moment)
    return (new_global, new_moment)


def on_device(
    inputs,
    doc_ids,
    values,
    cotangent,
    weights,
    moment1,
    moment2,
    frag_local,
    frag_global,
    frag_moment,
    frag_index,
):
    new_weights, new_moment1, new_moment2 = inner_step(
        inputs, doc_ids, values, cotangent, weights, moment1, moment2
    )
    new_global, new_moment = outer_step(frag_local, frag_global, frag_moment, frag_index)
    return (new_weights, new_moment1, new_moment2, new_global, new_moment)


def solution(mesh):
    placed = (
        P(("replica", "shard"), None),
        P(("replica", "shard"), None),
        P(("replica", "shard"), None),
        P(("replica", "shard"), None),
        P(("replica", "shard"), None),
        P(("replica", "shard"), None),
        P(("replica", "shard"), None),
        P("replica", None, "shard", None),
        P(None, "shard", None),
        P(None, "shard", None),
        P(),
    )
    return jax.shard_map(
        on_device,
        mesh=mesh,
        in_specs=placed,
        out_specs=(
            P(("replica", "shard"), None),
            P(("replica", "shard"), None),
            P(("replica", "shard"), None),
            P("shard", None),
            P("shard", None),
        ),
        check_vma=False,
    )
```

profile of v0, /device:TPU:6, one launch (start us, length us, event | category | flops | bytes accessed | tf_op | source)
XLA Modules:
  0.0 230.8 jit_solution(15409681742219302765)
XLA Ops:
  7.2 0.0 copy-start
  7.2 0.0 all-gather.2.cloned.1.call-start
  7.2 1.7 convert_element_type.43
  9.0 0.0 all-gather.2.cloned.1.call-update
  9.0 0.0 copy-start.5
  9.0 0.0 copy-start.3
  9.0 0.0 copy-start.4
  9.0 0.0 reduce-scatter.4.cloned.1.call-start
  9.1 75.2 %all-gather.2.cloned.1.call-done = bf16[6144,256]{1,0:T(8,128)(2,1)} async-done(((bf16[192,256]{1,0:T(8,128)(2,1)}), bf16[6144,256]{1,0:T(8,128)(2,1)}) %all-gather.2.cloned.1.call-update) | async-done | bytes 3145744 | tf_op jit(solution)/shard_map/all_gather | solution.py:56
  84.2 0.0 copy-done
  84.2 3.2 %convolution_multiply_fusion.1 = f32[256,256]{0,1:T(8,128)S(1)} fusion(bf16[256,6144]{1,0:T(8,128)(2,1)S(1)} %copy-done, bf16[6144,256]{1,0:T(8,128)(2,1)} %all-gather.2.cloned.1.call-done), kind=kOutput, calls=%fused_computation.5 | convolution fusion | flops 805371904 | bytes 6553600 | tf_op jit(solution)/shard_map/dot_general | solution.py:57
  87.5 0.0 copy-done.5
  87.5 0.4 fusion.20
  88.0 0.0 copy-done.3
  88.0 0.0 copy-done.4
  88.0 0.2 multiply_reduce_fusion
  88.2 0.4 fusion.9
  88.6 0.3 multiply_reduce_fusion.2
  89.0 0.1 subtract_multiply_fusion.1
  89.1 2.7 %fusion = bf16[6144,256]{0,1:T(8,128)(2,1)} fusion(bf16[256,6144]{1,0:T(8,128)(2,1)S(1)} %copy-done, f32[256,128]{0,1:T(8,128)S(1)} %get-tuple-element.25, f32[256,128]{0,1:T(8,128)S(1)} %get-tuple-element.24), kind=kOutput, calls=%fused_computation.1 | convolution fusion | flops 807075840 | bytes 6553600 | tf_op jit(solution)/shard_map/dot_general | solution.py:59
  91.8 4.6 %copy.31 = bf16[6144,256]{1,0:T(8,128)(2,1)} copy(bf16[6144,256]{0,1:T(8,128)(2,1)} %fusion) | data formatting | bytes 6291456
  96.4 0.0 copy-start.1
  96.4 0.0 copy-start.2
  96.4 0.0 reduce-scatter.4.cloned.1.call-update
  97.1 1.5 fusion.15
  98.7 79.4 %psum.7 = f32[1,6144]{1,0:T(1,128)} all-reduce(bf16[1,6144]{1,0:T(2,128)(2,1)} %fusion.15), channel_id=1, replica_groups=mesh['replica'=16,'shard'=32] {'replica'}, use_global_device_ids=true, to_apply=%region_7.8 | all-reduce | flops 6144 | bytes 36864 | tf_op jit(solution)/shard_map/psum | solution.py:85
  178.1 1.5 bitcast_subtract_fusion
  179.6 42.5 %reduce-scatter.4.cloned.1.call-done = bf16[192,256]{1,0:T(8,128)(2,1)} async-done(((bf16[6144,256]{1,0:T(8,128)(2,1)}), bf16[192,256]{1,0:T(8,128)(2,1)}) %reduce-scatter.4.cloned.1.call-update) | async-done | bytes 98320 | tf_op jit(solution)/shard_map/reduce_scatter | solution.py:62
  222.1 0.0 copy-done.1
  222.1 0.0 copy-done.2
  222.1 1.9 multiply_subtract_fusion
  (4 shorter events, 0.1 us)
Async XLA Ops:
  7.2 77.1 %copy-start = (bf16[256,6144]{1,0:T(8,128)(2,1)S(1)}, bf16[256,6144]{1,0:T(8,128)(2,1)}, u32[]{:S(2)}) copy-start(bf16[256,6144]{1,0:T(8,128)(2,1)} %param.11) | copy-start | bytes 9437188
  7.2 77.0 %all-gather.2.cloned.1.call-start = ((), (), s32[]{:S(2)}) async-start(), calls=%async_computation.1 | async-start | bytes 3244032 | tf_op jit(solution)/shard_map/all_gather | solution.py:56
  9.0 78.5 %copy-start.5 = (s32[1,256]{1,0:T(1,128)S(1)}, s32[1,256]{1,0:T(1,128)}, u32[]{:S(2)}) copy-start(s32[1,256]{1,0:T(1,128)} %param.12) | copy-start | bytes 3076
  9.0 79.0 %copy-start.3 = (bf16[256,128]{1,0:T(8,128)(2,1)S(1)}, bf16[256,128]{1,0:T(8,128)(2,1)}, u32[]{:S(2)}) copy-start(bf16[256,128]{1,0:T(8,128)(2,1)} %param.14) | copy-start | bytes 196612
  9.0 79.0 %copy-start.4 = (bf16[256,128]{1,0:T(8,128)(2,1)S(1)}, bf16[256,128]{1,0:T(8,128)(2,1)}, u32[]{:S(2)}) copy-start(bf16[256,128]{1,0:T(8,128)(2,1)} %param.13) | copy-start | bytes 196612
  9.0 213.1 %reduce-scatter.4.cloned.1.call-start = ((), (), s32[]{:S(2)}) async-start(), calls=%async_computation.2 | async-start | bytes 3244032 | tf_op jit(solution)/shard_map/reduce_scatter | solution.py:62
  96.4 125.7 %copy-start.1 = (f32[192,256]{1,0:T(8,128)S(1)}, f32[192,256]{1,0:T(8,128)}, u32[]{:S(2)}) copy-start(f32[192,256]{1,0:T(8,128)} %param.15) | copy-start | bytes 589828
  96.4 125.7 %copy-start.2 = (f32[192,256]{1,0:T(8,128)S(1)}, f32[192,256]{1,0:T(8,128)}, u32[]{:S(2)}) copy-start(f32[192,256]{1,0:T(8,128)} %param.16) | copy-start | bytes 589828
Sparse Core Ops, SparseCore 0:
  10.7 73.4 all-gather.1
  96.6 125.4 reduce-scatter.3
where the time goes:
time: 232 us; the launch traced here: 231 us
  waiting for transfers between devices  118 us (51%)
  blocking collectives  79.4 us (34%)
  between operations  14.8 us (6%)
  matrix products  7.36 us (3%)
  other arithmetic  6.72 us (3%)
  local copies, waits for them, and re-layouts  4.68 us (2%)
    psum x1, blocking collectives, outer_step(): drift_mean = lax.psum(drift, 'replica') / replicas  79.4 us
    all_gather x1, waiting for transfers between devices, inner_step(): gathered = lax.all_gather(lowered, 'shard', axis=0, tiled=True)  75.2 us
    reduce_scatter x1, waiting for transfers between devices, inner_step(): lax.psum_scatter(grad_term.astype(jnp.bfloat16), 'shard', scatter_dimensi...  42.5 us
    unnamed x13, local copies, waits for them, and re-layouts  4.68 us
  transfers between devices with their start and end apart: 2, of which 2 were waited for; matrix products, arithmetic and copies ran while one was open for 1% of the time, Pallas kernels for 0%

commit v1 on v0

v1 whole, which is shorter than its diff:
```python
import functools
import math

import jax
import jax.numpy as jnp
from jax import lax
from jax.experimental import pallas as pl
from jax.experimental.pallas import tpu as pltpu
from jax.sharding import PartitionSpec as P

ADAM_STEP = 100

epsilon = 1e-06
beta_one = 0.9
beta_two = 0.95
learn_rate = 0.01
decay_rate = 0.1
outer_momentum = 0.9
outer_rate = 0.7

Z = 8
DIRS = (1, -1)
KIND_A, KIND_B, KIND_O = 0, 1, 2
ORDER = (4, 3, -3, 2, -2, 1, -1, 0)


class Lanes:
    def __init__(self):
        self.numbers = {}

    def __call__(self, *key):
        return self.numbers.setdefault(key, len(self.numbers))


def kernel(
    n_x,
    n_y,
    lanes,
    index_ref,
    x_hbm,
    doc_hbm,
    val_hbm,
    cot_hbm,
    w_hbm,
    local_hbm,
    global_hbm,
    moment_hbm,
    grad_out,
    global_out,
    moment_out,
    x_buf,
    xt_buf,
    w_buf,
    gathered,
    proj,
    doc_buf,
    val_buf,
    cot_buf,
    allowed_buf,
    grad_att,
    gp_buf,
    local_buf,
    global_buf,
    moment_buf,
    drift_buf,
    x_recv,
    xsum_buf,
    y_recv,
    sums,
    chip_send,
    chip_recv,
    pair_send,
    pair_recv,
    ring_send,
    ring_recv,
    last_send,
    last_recv,
    load_sem,
    send_sem,
    recv_sem,
):
    tokens, width = x_buf.shape
    head = val_buf.shape[1]
    rows = width // (4 * Z)
    half, quarter = rows // 2, rows // 4

    replica = lax.axis_index("replica")
    shard = lax.axis_index("shard")
    my_x, my_y = replica // n_y, lax.rem(replica, n_y)
    side, z, core = shard // 16, lax.rem(shard // 2, Z), lax.rem(shard, 2)
    other = 1 - side

    def at_z(step):
        return lax.rem(z + step + 2 * Z, Z)

    def unit(col, zz, cc):
        return col * 16 + zz * 2 + cc

    to_core = {"shard": unit(side, z, 1 - core)}
    to_side = {"shard": unit(other, z, core)}
    to_z = {d: {"shard": unit(side, at_z(d), core)} for d in DIRS}
    to_x = [{"replica": lax.rem(my_x + k, n_x) * n_y + my_y} for k in range(1, n_x)]
    to_y = [{"replica": my_x * n_y + lax.rem(my_y + k, n_y)} for k in range(1, n_y)]

    started = []

    def send(key, src, dst, target):
        n = lanes(*key)
        copy = pltpu.make_async_remote_copy(
            src_ref=src,
            dst_ref=dst,
            send_sem=send_sem.at[n],
            recv_sem=recv_sem.at[n],
            device_id=target,
            device_id_type=pl.DeviceIdType.MESH,
        )
        copy.start()
        started.append(copy)

    def arrive(key, dst):
        n = lanes(*key)
        pltpu.make_async_remote_copy(
            src_ref=dst,
            dst_ref=dst,
            send_sem=send_sem.at[n],
            recv_sem=recv_sem.at[n],
            device_id=to_core,
            device_id_type=pl.DeviceIdType.MESH,
        ).wait_recv()

    def load(n, src, dst):
        copy = pltpu.make_async_copy(src, dst, load_sem.at[n])
        copy.start()
        return copy

    load_w = load(0, w_hbm, w_buf)
    load_local = load(1, local_hbm, local_buf)
    load_global = load(2, global_hbm, global_buf)
    load_x = load(3, x_hbm, x_buf)
    load_doc = load(4, doc_hbm, doc_buf)
    load_val = load(5, val_hbm, val_buf)
    load_cot = load(6, cot_hbm, cot_buf)
    load_moment = load(7, moment_hbm, moment_buf)

    barrier = pltpu.get_barrier_semaphore()
    partners = [to_core, to_side, to_z[1], to_z[-1]] + to_x + to_y
    for partner in partners:
        pl.semaphore_signal(
            barrier, inc=1, device_id=partner, device_id_type=pl.DeviceIdType.MESH
        )

    def span(col, zz, cc, lo, count):
        start = pl.multiple_of(unit(col, zz, cc) * rows + lo, 16)
        return gathered.at[pl.ds(start, count), :]

    load_w.wait()
    span(side, z, core, 0, rows)[...] = w_buf[...].astype(jnp.bfloat16)

    chosen = index_ref[0]
    load_local.wait()
    load_global.wait()
    current = global_buf[chosen]
    local_rows = local_buf[...].astype(jnp.float32)
    picked = lax.broadcasted_iota(jnp.int32, local_rows.shape, 0) == chosen
    local_copy = jnp.sum(jnp.where(picked, local_rows, 0.0), axis=0, keepdims=True)
    drift_buf[...] = (current - local_copy).astype(jnp.bfloat16).astype(jnp.float32)

    pl.semaphore_wait(barrier, len(partners))

    def piece(kind, direction, d, cc):
        zz = at_z(-direction * d)
        col = other if kind == KIND_O else side
        lo = 0 if kind == KIND_A else half
        if d == 4:
            return span(col, zz, cc, lo + (0 if direction == 1 else quarter), quarter)
        return span(col, zz, cc, lo, half)

    def side_piece(direction, d, cc, col):
        zz = at_z(-direction * d)
        if d == 4:
            return span(col, zz, cc, 0 if direction == 1 else quarter, quarter)
        return span(col, zz, cc, 0, half)

    def ring_on(kind, direction, d):
        if d < 4:
            src = piece(kind, direction, d, core)
            if d == 3:
                zz = at_z(-direction * d)
                col = other if kind == KIND_O else side
                lo = 0 if kind == KIND_A else half
                src = span(col, zz, core, lo + (0 if direction == 1 else quarter), quarter)
            send(("ring", kind, direction, d + 1), src, src, to_z[direction])

    for direction in DIRS:
        ring_on(KIND_A, direction, 0)
    first_b = span(side, z, core, half, half)
    send(("sideB",), first_b, first_b, to_side)
    for direction in DIRS:
        ring_on(KIND_B, direction, 0)
    first_a = span(side, z, core, 0, half)
    send(("sideA", 0, 1), first_a, first_a, to_side)
    mine = span(side, z, core, 0, rows)
    send(("core", "own"), mine, mine, to_core)
    for k, target in enumerate(to_x):
        send(("x", k), drift_buf, x_recv.at[k], target)

    load_x.wait()
    block = 2 * rows

    def transpose_block(p):
        cols = slice(p * block, (p + 1) * block)
        xt_buf[cols, :] = x_buf[:, cols].T

    def make_allowed():
        load_doc.wait()
        by_column = jnp.broadcast_to(doc_buf[...], (tokens, tokens))
        by_row = by_column.T
        row = lax.broadcasted_iota(jnp.int32, (tokens, tokens), 0)
        column = lax.broadcasted_iota(jnp.int32, (tokens, tokens), 1)
        same = (by_row == by_column) & (column <= row)
        allowed_buf[...] = jnp.where(same, 1.0, 0.0)

    def make_grad_att():
        load_val.wait()
        load_cot.wait()
        grad_att[...] = lax.dot_general(
            cot_buf[...],
            val_buf[...],
            (((1,), (1,)), ((), ())),
            preferred_element_type=jnp.float32,
        )

    def multiply(col, zz, first=False):
        start = pl.multiple_of(unit(col, zz, 0) * rows, 128)
        term = jnp.dot(
            x_buf[:, pl.ds(start, block)],
            gathered[pl.ds(start, block), :],
            preferred_element_type=jnp.float32,
        )
        if first:
            proj[...] = term
        else:
            proj[...] += term

    def arrive_core(d):
        for direction in DIRS if d else (1,):
            if d == 0:
                arrive(("core", "own"), span(side, z, 1 - core, 0, rows))
                arrive(("core", "sideB"), span(other, z, 1 - core, half, half))
            else:
                for kind in (KIND_A, KIND_B, KIND_O):
                    arrive(
                        ("core", kind, direction, d), piece(kind, direction, d, 1 - core)
                    )
            arrive(
                ("core", "sideA", direction, d), side_piece(direction, d, 1 - core, other)
            )

    fillers = [functools.partial(transpose_block, p) for p in range(2 * Z)]
    fillers += [make_allowed, make_grad_att]

    def fill(count=1):
        for _ in range(min(count, len(fillers))):
            fillers.pop(0)()

    def queue_products(d):
        def first_of(d=d):
            arrive_core(d)

        fillers.append(first_of)
        for direction in DIRS if 0 < d < 4 else (1,):
            for col in (side, other):
                fillers.append(
                    functools.partial(
                        multiply, col, at_z(-direction * d), first=d == 0 and col is side
                    )
                )

    def sums_over_x():
        total = drift_buf[...]
        for k in range(n_x - 1):
            arrive(("x", k), x_recv.at[k])
            total = total + x_recv[k]
        xsum_buf[...] = total
        for k, target in enumerate(to_y):
            send(("y", k), xsum_buf, y_recv.at[k], target)

    arrive(("sideB",), span(other, z, core, half, half))
    for direction in DIRS:
        ring_on(KIND_O, direction, 0)
    their_b = span(other, z, core, half, half)
    send(("core", "sideB"), their_b, their_b, to_core)
    fill(4)
    for d in range(1, 5):
        for kind in (KIND_A, KIND_B, KIND_O):
            for direction in DIRS:
                got = piece(kind, direction, d, core)
                arrive(("ring", kind, direction, d), got)
                ring_on(kind, direction, d)
                if kind == KIND_A:
                    send(("sideA", d, direction), got, got, to_side)
                send(("core", kind, direction, d), got, got, to_core)
            if kind == KIND_A:
                for direction in DIRS if d > 1 else (1,):
                    got = side_piece(direction, d - 1, core, other)
                    arrive(("sideA", d - 1, direction), got)
                    send(("core", "sideA", direction, d - 1), got, got, to_core)
            fill(2)
        if d >= 2:
            queue_products(d - 2)
    sums_over_x()
    fill(len(fillers))
    for direction in DIRS:
        got = side_piece(direction, 4, core, other)
        arrive(("sideA", 4, direction), got)
        send(("core", "sideA", direction, 4), got, got, to_core)
    queue_products(3)
    queue_products(4)
    fill(len(fillers))

    input_scale = 1.0 / math.sqrt(width)
    score_scale = 1.0 / math.sqrt(head)
    exact = lax.Precision.HIGHEST
    scaled = proj[...] * input_scale
    queries, keys_part = scaled[:, :head], scaled[:, head:]
    q_rate = lax.rsqrt(jnp.mean(queries * queries, axis=1, keepdims=True) + epsilon)
    k_rate = lax.rsqrt(jnp.mean(keys_part * keys_part, axis=1, keepdims=True) + epsilon)
    q_unit, k_unit = queries * q_rate, keys_part * k_rate
    scores = (
        lax.dot_general(
            q_unit,
            k_unit,
            (((1,), (1,)), ((), ())),
            precision=exact,
            preferred_element_type=jnp.float32,
        )
        * score_scale
    )
    raised = jnp.where(allowed_buf[...] > 0.5, jnp.exp(scores), 0.0)
    attention = raised / jnp.sum(raised, axis=1, keepdims=True)
    weighted = attention * grad_att[...]
    grad_scores = (
        weighted - attention * jnp.sum(weighted, axis=1, keepdims=True)
    ) * score_scale
    grad_qunit = jnp.dot(
        grad_scores, k_unit, precision=exact, preferred_element_type=jnp.float32
    )
    grad_kunit = jnp.dot(
        grad_scores.T, q_unit, precision=exact, preferred_element_type=jnp.float32
    )
    grad_query = q_rate * (
        grad_qunit - q_unit * jnp.mean(grad_qunit * q_unit, axis=1, keepdims=True)
    )
    grad_keys = k_rate * (
        grad_kunit - k_unit * jnp.mean(grad_kunit * k_unit, axis=1, keepdims=True)
    )
    gp_buf[:, :head] = (grad_query * input_scale).astype(jnp.bfloat16)
    gp_buf[:, head:] = (grad_keys * input_scale).astype(jnp.bfloat16)

    def place(delta):
        return ORDER.index(delta)

    def partial(col, zz, cc):
        start = pl.multiple_of(unit(col, zz, cc) * rows, 64)
        return jnp.dot(
            xt_buf[pl.ds(start, rows), :], gp_buf[...], preferred_element_type=jnp.float32
        )

    def compute(delta):
        i, zz = place(delta), at_z(delta)
        for k, col in ((1, other), (0, side)):
            chip_send[i, k] = partial(col, zz, 1 - core).astype(jnp.bfloat16)
            send(("chip", i, k), chip_send.at[i, k], chip_recv.at[i, k], to_core)
        for k, col in ((1, other), (0, side)):
            sums[i, k] = partial(col, zz, core)

    def pair(delta):
        i = place(delta)
        for k in (1, 0):
            arrive(("chip", i, k), chip_recv.at[i, k])
            sums[i, k] += chip_recv[i, k].astype(jnp.float32)
            if k == 1:
                pair_send[i] = sums[i, 1, :half].astype(jnp.bfloat16)
                send(("pair", i), pair_send.at[i], pair_recv.at[i], to_side)

    def across(delta):
        i = place(delta)
        arrive(("pair", i), pair_recv.at[i])
        sums[i, 0, :half] += pair_recv[i].astype(jnp.float32)

    def early(direction):
        return 1 if direction == 1 else 0

    def slot(direction, kind, d, h):
        return ((0 if direction == 1 else 1) * 3 + kind) * 8 + (d - 1) * 2 + h

    def ring_sum(kind, direction, d, h):
        delta = 4 if d == 4 else direction * d
        k = 1 if kind == KIND_O else 0
        lo = (0 if kind == KIND_A else half) + h * quarter
        total = sums[place(delta), k, lo : lo + quarter]
        if d < 3 or (d == 3 and h != early(direction)):
            n = slot(direction, kind, d + 1, h)
            arrive(("sum", n), ring_recv.at[n])
            total = total + ring_recv[n].astype(jnp.float32)
        n = slot(direction, kind, d, h)
        ring_send[n] = total.astype(jnp.bfloat16)
        send(("sum", n), ring_send.at[n], ring_recv.at[n], to_z[direction])

    compute(4)
    compute(3)
    compute(-3)
    pair(4)
    for kind in (KIND_O, KIND_B):
        for direction in DIRS:
            ring_sum(kind, direction, 4, 1 - early(direction))
    for direction in DIRS:
        pair(3 * direction)
        for kind in (KIND_O, KIND_B):
            ring_sum(kind, direction, 3, early(direction))
    compute(2)
    across(4)
    for direction in DIRS:
        ring_sum(KIND_A, direction, 4, 1 - early(direction))
    compute(-2)
    for direction in DIRS:
        across(3 * direction)
        ring_sum(KIND_A, direction, 3, early(direction))
    pair(2)
    pair(-2)
    compute(1)
    compute(-1)
    for kind in (KIND_O, KIND_B, KIND_A):
        for direction in DIRS:
            ring_sum(kind, direction, 3, 1 - early(direction))
    pair(1)
    pair(-1)
    compute(0)
    across(2)
    across(-2)
    for first in (True, False):
        for kind in (KIND_O, KIND_B, KIND_A):
            for direction in DIRS:
                h = early(direction) if first else 1 - early(direction)
                ring_sum(kind, direction, 2, h)
    pair(0)
    across(1)
    across(-1)
    for first in (True, False):
        for kind in (KIND_O, KIND_B, KIND_A):
            for direction in DIRS:
                h = early(direction) if first else 1 - early(direction)
                ring_sum(kind, direction, 1, h)

    load_moment.wait()
    total = xsum_buf[...]
    for k in range(n_y - 1):
        arrive(("y", k), y_recv.at[k])
        total = total + y_recv[k]
    drift_mean = total / (n_x * n_y)
    new_moment = outer_momentum * moment_buf[chosen] + drift_mean
    moment_out[...] = new_moment
    global_out[...] = global_buf[chosen] - outer_rate * (
        drift_mean + outer_momentum * new_moment
    )

    across(0)

    def last_sum(kind, h):
        k = 1 if kind == KIND_O else 0
        lo = (0 if kind == KIND_A else half) + h * quarter
        total = sums[place(0), k, lo : lo + quarter]
        for direction in DIRS:
            n = slot(direction, kind, 1, h)
            arrive(("sum", n), ring_recv.at[n])
            total = total + ring_recv[n].astype(jnp.float32)
        return total

    for h in (0, 1):
        last_send[h] = last_sum(KIND_O, h).astype(jnp.bfloat16)
        send(("last", h), last_send.at[h], last_recv.at[h], to_side)
    for h in (0, 1):
        grad_out[pl.ds(h * quarter, quarter), :] = last_sum(KIND_A, h)
    for h in (0, 1):
        total = last_sum(KIND_B, h)
        arrive(("last", h), last_recv.at[h])
        grad_out[pl.ds(half + h * quarter, quarter), :] = total + last_recv[h].astype(
            jnp.float32
        )
    for copy in started:
        copy.wait_send()


def exchange(n_replica, inputs, doc_ids, values, cotangent, weights, local, current, moment, index):
    tokens, width = inputs.shape
    head = values.shape[1]
    rows = width // (4 * Z)
    half, quarter = rows // 2, rows // 4
    n_x = min(4, n_replica)
    n_y = n_replica // n_x
    bf16, f32 = jnp.bfloat16, jnp.float32
    anywhere = pl.BlockSpec(memory_space=pl.ANY)
    vmem = pl.BlockSpec(memory_space=pltpu.VMEM)
    n_sem = 192
    return pl.pallas_call(
        functools.partial(kernel, n_x, n_y, Lanes()),
        out_shape=(
            jax.ShapeDtypeStruct((rows, 2 * head), f32),
            jax.ShapeDtypeStruct((1, width), f32),
            jax.ShapeDtypeStruct((1, width), f32),
        ),
        in_specs=[pl.BlockSpec(memory_space=pltpu.SMEM)] + [anywhere] * 8,
        out_specs=(vmem, vmem, vmem),
        scratch_shapes=[
            pltpu.VMEM((tokens, width), bf16),
            pltpu.VMEM((width, tokens), bf16),
            pltpu.VMEM((rows, 2 * head), f32),
            pltpu.VMEM((width, 2 * head), bf16),
            pltpu.VMEM((tokens, 2 * head), f32),
            pltpu.VMEM((1, tokens), jnp.int32),
            pltpu.VMEM((tokens, head), bf16),
            pltpu.VMEM((tokens, head), bf16),
            pltpu.VMEM((tokens, tokens), f32),
            pltpu.VMEM((tokens, tokens), f32),
            pltpu.VMEM((tokens, 2 * head), bf16),
            pltpu.VMEM(local.shape, bf16),
            pltpu.VMEM(current.shape, f32),
            pltpu.VMEM(moment.shape, f32),
            pltpu.VMEM((1, width), f32),
            pltpu.VMEM((max(n_x - 1, 1), 1, width), f32),
            pltpu.VMEM((1, width), f32),
            pltpu.VMEM((max(n_y - 1, 1), 1, width), f32),
            pltpu.VMEM((8, 2, rows, 2 * head), f32),
            pltpu.VMEM((8, 2, rows, 2 * head), bf16),
            pltpu.VMEM((8, 2, rows, 2 * head), bf16),
            pltpu.VMEM((8, half, 2 * head), bf16),
            pltpu.VMEM((8, half, 2 * head), bf16),
            pltpu.VMEM((48, quarter, 2 * head), bf16),
            pltpu.VMEM((48, quarter, 2 * head), bf16),
            pltpu.VMEM((2, quarter, 2 * head), bf16),
            pltpu.VMEM((2, quarter, 2 * head), bf16),
            pltpu.SemaphoreType.DMA((8,)),
            pltpu.SemaphoreType.DMA((n_sem,)),
            pltpu.SemaphoreType.DMA((n_sem,)),
        ],
        compiler_params=pltpu.CompilerParams(
            collective_id=0, has_side_effects=True, vmem_limit_bytes=56 * 1024 * 1024
        ),
    )(index, inputs, doc_ids, values, cotangent, weights, local, current, moment)


def on_device(
    n_replica,
    inputs,
    doc_ids,
    values,
    cotangent,
    weights,
    moment1,
    moment2,
    frag_local,
    frag_global,
    frag_moment,
    frag_index,
):
    gradient, new_global, new_moment = exchange(
        n_replica,
        inputs,
        doc_ids,
        values,
        cotangent,
        weights,
        frag_local[0, :, 0, :],
        frag_global,
        frag_moment,
        frag_index,
    )
    first_new = beta_one * moment1 + (1.0 - beta_one) * gradient
    second_new = beta_two * moment2 + (1.0 - beta_two) * gradient * gradient
    first_hat = first_new / (1.0 - beta_one**ADAM_STEP)
    second_hat = second_new / (1.0 - beta_two**ADAM_STEP)
    weight_new = weights - learn_rate * (
        first_hat / (jnp.sqrt(second_hat) + 1e-08) + decay_rate * weights
    )
    return (weight_new, first_new, second_new, new_global, new_moment)


def solution(mesh):
    both = P(("replica", "shard"), None)
    return jax.shard_map(
        functools.partial(on_device, mesh.shape["replica"]),
        mesh=mesh,
        in_specs=(both,) * 7
        + (
            P("replica", None, "shard", None),
            P(None, "shard", None),
            P(None, "shard", None),
            P(),
        ),
        out_specs=(both, both, both, P("shard", None), P("shard", None)),
        check_vma=False,
    )
```

time: 232 us -> 67.9 us (0.29)
  waiting for transfers between devices: 118 us -> 0 us
  blocking collectives: 79.4 us -> 0 us
  Pallas kernels: 0 us -> 61.7 us
  between operations: 14.8 us -> 1.4 us
  matrix products: 7.36 us -> 0 us
  other arithmetic: 6.72 us -> 1.82 us
    psum x1 -> x0, blocking collectives: 79.4 us -> none  [outer_step(): drift_mean = lax.psum(drift, 'replica') / replicas]
    all_gather x1 -> x0, waiting for transfers between devices: 75.2 us -> none  [inner_step(): gathered = lax.all_gather(lowered, 'shard', axis=0, tiled=True)]
    pallas_call x0 -> x1, Pallas kernels: none -> 61.7 us  [exchange(): pl.pallas_call(functools.partial(kernel, n_x, n_y, Lanes()), out_shape=(j...]
    reduce_scatter x1 -> x0, waiting for transfers between devices: 42.5 us -> none  [inner_step(): lax.psum_scatter(grad_term.astype(jnp.bfloat16), 'shard', scatter_dimensi...]
    dot_general x6 -> x0, matrix products: 7.36 us -> none  [the longest x1 3.22 us: inner_step(): projected = jnp.dot(inputs, gathered, preferred_element_type=jnp.float32)]
    convert_element_type x2 -> x0, other arithmetic: 3.27 us -> none  [the longest x1 1.73 us: inner_step(): lowered = weights.astype(jnp.bfloat16)]
    unnamed x13 -> x8, local copies, waits for them, and re-layouts: 4.68 us -> 2.7 us
  transfers between devices with their start and end apart: 2 -> 0, of which waited for: 2 -> 0; matrix products, arithmetic and copies ran while one was open for 1% -> 0% of each run, Pallas kernels for 0% -> 0%
where the time goes in v1:
time: 67.9 us; the launch traced here: 67.6 us
  Pallas kernels  61.7 us (91%)
  local copies, waits for them, and re-layouts  2.7 us (4%)
  other arithmetic  1.82 us (3%)
  between operations  1.4 us (2%)
    pallas_call x1, Pallas kernels, exchange(): pl.pallas_call(functools.partial(kernel, n_x, n_y, Lanes()), out_shape=(j...  61.7 us
    unnamed x8, local copies, waits for them, and re-layouts  2.7 us
    sub x1, other arithmetic, on_device(): weights - learn_rate * (first_hat / (jnp.sqrt(second_hat) + 1e-08) + deca...  1.82 us

profile of v1, /device:TPU:6, one launch (start us, length us, event | category | flops | bytes accessed | tf_op | source)
XLA Modules:
  0.0 67.6 jit_solution(7555806473101563356)
XLA Ops:
  0.6 0.0 copy-start
  0.6 0.0 copy-start.2
  0.7 0.0 copy-start.1
  1.4 61.7 %shard_map.146 = (f32[192,256]{1,0:T(8,128)}, f32[1,6144]{1,0:T(1,128)}, f32[1,6144]{1,0:T(1,128)}) custom-call(s32[1]{0:T(128)S(6)} %copy.18.index_ref, bf16[256,6144]{1,0:T(8,128)(2,1)} %x_hbm.1, s32[1,256]{1,0:T(1,128)} %doc_hbm.1, bf16[256,128]{1,0:T(8,128)(2,1)} %val_hbm.1, bf16[256,128]{1,0:T(8,128)(2,1)} %cot_hbm.1, f32[192,256]{1,0:T(8,128)} %w_hbm.1, ...), custom_call_target="tpu_custom_call" | custom-call | tf_op jit(solution)/shard_map/pallas_call | solution.py:505
  63.1 0.0 copy-done
  63.1 0.0 copy-done.2
  63.1 0.0 copy-done.1
  63.1 1.8 %multiply_subtract_fusion = (f32[192,256]{1,0:T(8,128)}, f32[192,256]{1,0:T(8,128)}, f32[192,256]{1,0:T(8,128)}) fusion(f32[192,256]{1,0:T(8,128)S(1)} %copy-done, f32[192,256]{1,0:T(8,128)} %get-tuple-element.8, f32[192,256]{1,0:T(8,128)S(1)} %copy-done.1, f32[192,256]{1,0:T(8,128)S(1)} %copy-done.2), kind=kLoop, calls=%fused_computation.2 | loop fusion | flops 737280 | bytes 1376256 | tf_op jit(solution)/shard_map/sub | solution.py:582
  64.9 1.3 %copy.19 = f32[1,6144]{1,0:T(1,128)} copy(f32[1,6144]{1,0:T(1,128)} %get-tuple-element.22) | data formatting | bytes 49152
  66.3 1.3 %copy.20 = f32[1,6144]{1,0:T(1,128)} copy(f32[1,6144]{1,0:T(1,128)} %get-tuple-element.23) | data formatting | bytes 49152
Async XLA Ops:
  0.6 62.5 %copy-start = (f32[192,256]{1,0:T(8,128)S(1)}, f32[192,256]{1,0:T(8,128)}, u32[]{:S(2)}) copy-start(f32[192,256]{1,0:T(8,128)} %w_hbm.1) | copy-start | bytes 589828
  0.6 62.5 %copy-start.2 = (f32[192,256]{1,0:T(8,128)S(1)}, f32[192,256]{1,0:T(8,128)}, u32[]{:S(2)}) copy-start(f32[192,256]{1,0:T(8,128)} %param.17) | copy-start | bytes 589828
  0.7 62.5 %copy-start.1 = (f32[192,256]{1,0:T(8,128)S(1)}, f32[192,256]{1,0:T(8,128)}, u32[]{:S(2)}) copy-start(f32[192,256]{1,0:T(8,128)} %param.16) | copy-start | bytes 589828

commit v2 on v1

--- a/solution.py
+++ b/solution.py
@@ -21,6 +21,7 @@
 Z = 8
 DIRS = (1, -1)
 KIND_A, KIND_B, KIND_O = 0, 1, 2
+RING, SIDE, CORE, CHIP, PAIR, SUM, LAST, ACROSS_X, ACROSS_Y = range(9)
 ORDER = (4, 3, -3, 2, -2, 1, -1, 0)
 
 
@@ -36,7 +37,7 @@
     n_x,
     n_y,
     lanes,
-    index_ref,
+    index_hbm,
     x_hbm,
     doc_hbm,
     val_hbm,
@@ -48,6 +49,7 @@
     grad_out,
     global_out,
     moment_out,
+    index_buf,
     x_buf,
     xt_buf,
     w_buf,
@@ -102,31 +104,31 @@
     to_x = [{"replica": lax.rem(my_x + k, n_x) * n_y + my_y} for k in range(1, n_x)]
     to_y = [{"replica": my_x * n_y + lax.rem(my_y + k, n_y)} for k in range(1, n_y)]
 
-    started = []
-
-    def send(key, src, dst, target):
-        n = lanes(*key)
-        copy = pltpu.make_async_remote_copy(
+    def describe(stream, key, src, dst, target):
+        return pltpu.make_async_remote_copy(
             src_ref=src,
             dst_ref=dst,
-            send_sem=send_sem.at[n],
-            recv_sem=recv_sem.at[n],
+            send_sem=send_sem.at[stream],
+            recv_sem=recv_sem.at[lanes(*key)],
             device_id=target,
             device_id_type=pl.DeviceIdType.MESH,
         )
-        copy.start()
-        started.append(copy)
+
+    def send(stream, key, src, dst, target):
+        describe(stream, key, src, dst, target).start()
 
     def arrive(key, dst):
-        n = lanes(*key)
-        pltpu.make_async_remote_copy(
-            src_ref=dst,
-            dst_ref=dst,
-            send_sem=send_sem.at[n],
-            recv_sem=recv_sem.at[n],
-            device_id=to_core,
-            device_id_type=pl.DeviceIdType.MESH,
-        ).wait_recv()
+        describe(0, key, dst, dst, to_core).wait_recv()
+
+    def drain(stream, src):
+        describe(stream, ("core", 0), src, src, to_core).wait_send()
+
+    barrier = pltpu.get_barrier_semaphore()
+    partners = [to_core, to_side, to_z[1], to_z[-1]] + to_x + to_y
+    for partner in partners:
+        pl.semaphore_signal(
+            barrier, inc=1, device_id=partner, device_id_type=pl.DeviceIdType.MESH
+        )
 
     def load(n, src, dst):
         copy = pltpu.make_async_copy(src, dst, load_sem.at[n])
@@ -141,13 +143,7 @@
     load_val = load(5, val_hbm, val_buf)
     load_cot = load(6, cot_hbm, cot_buf)
     load_moment = load(7, moment_hbm, moment_buf)
-
-    barrier = pltpu.get_barrier_semaphore()
-    partners = [to_core, to_side, to_z[1], to_z[-1]] + to_x + to_y
-    for partner in partners:
-        pl.semaphore_signal(
-            barrier, inc=1, device_id=partner, device_id_type=pl.DeviceIdType.MESH
-        )
+    load_index = load(8, index_hbm, index_buf)
 
     def span(col, zz, cc, lo, count):
         start = pl.multiple_of(unit(col, zz, cc) * rows + lo, 16)
@@ -156,7 +152,8 @@
     load_w.wait()
     span(side, z, core, 0, rows)[...] = w_buf[...].astype(jnp.bfloat16)
 
-    chosen = index_ref[0]
+    load_index.wait()
+    chosen = index_buf[0]
     load_local.wait()
     load_global.wait()
     current = global_buf[chosen]
@@ -189,27 +186,36 @@
                 col = other if kind == KIND_O else side
                 lo = 0 if kind == KIND_A else half
                 src = span(col, zz, core, lo + (0 if direction == 1 else quarter), quarter)
-            send(("ring", kind, direction, d + 1), src, src, to_z[direction])
-
+            send(RING, ("ring", kind, direction, d + 1), src, src, to_z[direction])
+
+    def side_on(d, got):
+        send(SIDE, ("side", d), got, got, to_side)
+
+    def core_on(d, got):
+        send(CORE, ("core", d), got, got, to_core)
+
+    first_a = span(side, z, core, 0, half)
+    first_b = span(side, z, core, half, half)
+    their_b = span(other, z, core, half, half)
     for direction in DIRS:
         ring_on(KIND_A, direction, 0)
-    first_b = span(side, z, core, half, half)
-    send(("sideB",), first_b, first_b, to_side)
+    send(SIDE, ("sideB",), first_b, first_b, to_side)
     for direction in DIRS:
         ring_on(KIND_B, direction, 0)
-    first_a = span(side, z, core, 0, half)
-    send(("sideA", 0, 1), first_a, first_a, to_side)
-    mine = span(side, z, core, 0, rows)
-    send(("core", "own"), mine, mine, to_core)
+    side_on(0, first_a)
+    core_on(0, span(side, z, core, 0, rows))
     for k, target in enumerate(to_x):
-        send(("x", k), drift_buf, x_recv.at[k], target)
+        send(ACROSS_X, ("x",), drift_buf, x_recv.at[k], target)
 
     load_x.wait()
     block = 2 * rows
 
     def transpose_block(p):
         cols = slice(p * block, (p + 1) * block)
-        xt_buf[cols, :] = x_buf[:, cols].T
+        turned = x_buf[:, cols].T
+        for cc in (0, 1):
+            start = pl.multiple_of(p * block + (core if cc == 0 else 1 - core) * rows, 64)
+            xt_buf[pl.ds(start, rows), :] = turned[cc * rows : (cc + 1) * rows]
 
     def make_allowed():
         load_doc.wait()
@@ -243,18 +249,8 @@
             proj[...] += term
 
     def arrive_core(d):
-        for direction in DIRS if d else (1,):
-            if d == 0:
-                arrive(("core", "own"), span(side, z, 1 - core, 0, rows))
-                arrive(("core", "sideB"), span(other, z, 1 - core, half, half))
-            else:
-                for kind in (KIND_A, KIND_B, KIND_O):
-                    arrive(
-                        ("core", kind, direction, d), piece(kind, direction, d, 1 - core)
-                    )
-            arrive(
-                ("core", "sideA", direction, d), side_piece(direction, d, 1 - core, other)
-            )
+        count = 2 * rows if d in (0, 4) else 4 * rows
+        arrive(("core", d), gathered.at[pl.ds(0, count), :])
 
     fillers = [functools.partial(transpose_block, p) for p in range(2 * Z)]
     fillers += [make_allowed, make_grad_att]
@@ -264,10 +260,7 @@
             fillers.pop(0)()
 
     def queue_products(d):
-        def first_of(d=d):
-            arrive_core(d)
-
-        fillers.append(first_of)
+        fillers.append(functools.partial(arrive_core, d))
         for direction in DIRS if 0 < d < 4 else (1,):
             for col in (side, other):
                 fillers.append(
@@ -278,43 +271,46 @@
 
     def sums_over_x():
         total = drift_buf[...]
+        if n_x > 1:
+            arrive(("x",), x_recv)
         for k in range(n_x - 1):
-            arrive(("x", k), x_recv.at[k])
             total = total + x_recv[k]
         xsum_buf[...] = total
         for k, target in enumerate(to_y):
-            send(("y", k), xsum_buf, y_recv.at[k], target)
-
-    arrive(("sideB",), span(other, z, core, half, half))
-    for direction in DIRS:
-        ring_on(KIND_O, direction, 0)
-    their_b = span(other, z, core, half, half)
-    send(("core", "sideB"), their_b, their_b, to_core)
-    fill(4)
+            send(ACROSS_Y, ("y",), xsum_buf, y_recv.at[k], target)
+
+    def from_side(d):
+        arrive(("side", d), gathered.at[pl.ds(0, half if d in (0, 4) else rows), :])
+        for direction in DIRS if d else (1,):
+            core_on(d, side_piece(direction, d, core, other))
+
+    def from_ring(kind, d):
+        for direction in DIRS:
+            got = piece(kind, direction, d, core)
+            arrive(("ring", kind, direction, d), got)
+            ring_on(kind, direction, d)
+            if kind == KIND_A:
+                side_on(d, got)
+            core_on(d, got)
+
+    fill(2)
     for d in range(1, 5):
-        for kind in (KIND_A, KIND_B, KIND_O):
+        from_ring(KIND_A, d)
+        from_ring(KIND_B, d)
+        if d == 1:
+            arrive(("sideB",), their_b)
             for direction in DIRS:
-                got = piece(kind, direction, d, core)
-                arrive(("ring", kind, direction, d), got)
-                ring_on(kind, direction, d)
-                if kind == KIND_A:
-                    send(("sideA", d, direction), got, got, to_side)
-                send(("core", kind, direction, d), got, got, to_core)
-            if kind == KIND_A:
-                for direction in DIRS if d > 1 else (1,):
-                    got = side_piece(direction, d - 1, core, other)
-                    arrive(("sideA", d - 1, direction), got)
-                    send(("core", "sideA", direction, d - 1), got, got, to_core)
-            fill(2)
-        if d >= 2:
-            queue_products(d - 2)
+                ring_on(KIND_O, direction, 0)
+            core_on(0, their_b)
+        else:
+            from_ring(KIND_O, d - 1)
+        fill(3)
+        from_side(d - 1)
+        fill(3)
+        queue_products(d - 1)
     sums_over_x()
-    fill(len(fillers))
-    for direction in DIRS:
-        got = side_piece(direction, 4, core, other)
-        arrive(("sideA", 4, direction), got)
-        send(("core", "sideA", direction, 4), got, got, to_core)
-    queue_products(3)
+    from_side(4)
+    from_ring(KIND_O, 4)
     queue_products(4)
     fill(len(fillers))
 
@@ -360,28 +356,27 @@
     def place(delta):
         return ORDER.index(delta)
 
-    def partial(col, zz, cc):
-        start = pl.multiple_of(unit(col, zz, cc) * rows, 64)
-        return jnp.dot(
-            xt_buf[pl.ds(start, rows), :], gp_buf[...], preferred_element_type=jnp.float32
-        )
-
     def compute(delta):
         i, zz = place(delta), at_z(delta)
         for k, col in ((1, other), (0, side)):
-            chip_send[i, k] = partial(col, zz, 1 - core).astype(jnp.bfloat16)
-            send(("chip", i, k), chip_send.at[i, k], chip_recv.at[i, k], to_core)
-        for k, col in ((1, other), (0, side)):
-            sums[i, k] = partial(col, zz, core)
+            start = pl.multiple_of(unit(col, zz, 0) * rows, 128)
+            term = jnp.dot(
+                xt_buf[pl.ds(start, block), :],
+                gp_buf[...],
+                preferred_element_type=jnp.float32,
+            )
+            chip_send[i, k] = term[rows:].astype(jnp.bfloat16)
+            sums[i, k] = term[:rows]
+        send(CHIP, ("chip", i), chip_send.at[i], chip_recv.at[i], to_core)
 
     def pair(delta):
         i = place(delta)
+        arrive(("chip", i), chip_recv.at[i])
         for k in (1, 0):
-            arrive(("chip", i, k), chip_recv.at[i, k])
             sums[i, k] += chip_recv[i, k].astype(jnp.float32)
             if k == 1:
                 pair_send[i] = sums[i, 1, :half].astype(jnp.bfloat16)
-                send(("pair", i), pair_send.at[i], pair_recv.at[i], to_side)
+                send(PAIR, ("pair", i), pair_send.at[i], pair_recv.at[i], to_side)
 
     def across(delta):
         i = place(delta)
@@ -405,64 +400,69 @@
             total = total + ring_recv[n].astype(jnp.float32)
         n = slot(direction, kind, d, h)
         ring_send[n] = total.astype(jnp.bfloat16)
-        send(("sum", n), ring_send.at[n], ring_recv.at[n], to_z[direction])
-
+        send(SUM, ("sum", n), ring_send.at[n], ring_recv.at[n], to_z[direction])
+
+    def sum_on(kinds, d, first, directions=DIRS):
+        for kind in kinds:
+            for direction in directions:
+                h = early(direction) if first else 1 - early(direction)
+                ring_sum(kind, direction, d, h)
+
+    whole, split = (KIND_O, KIND_B), (KIND_A,)
     compute(4)
     compute(3)
+    pair(4)
+    sum_on(whole, 4, False)
     compute(-3)
-    pair(4)
-    for kind in (KIND_O, KIND_B):
-        for direction in DIRS:
-            ring_sum(kind, direction, 4, 1 - early(direction))
-    for direction in DIRS:
-        pair(3 * direction)
-        for kind in (KIND_O, KIND_B):
-            ring_sum(kind, direction, 3, early(direction))
+    pair(3)
+    sum_on(whole, 3, True, (1,))
     compute(2)
+    pair(-3)
+    sum_on(whole, 3, True, (-1,))
+    compute(-2)
+    pair(2)
+    sum_on(whole, 3, False)
+    compute(1)
+    pair(-2)
     across(4)
-    for direction in DIRS:
-        ring_sum(KIND_A, direction, 4, 1 - early(direction))
-    compute(-2)
-    for direction in DIRS:
-        across(3 * direction)
-        ring_sum(KIND_A, direction, 3, early(direction))
-    pair(2)
-    pair(-2)
-    compute(1)
+    sum_on(split, 4, False)
+    sum_on(whole, 2, True)
     compute(-1)
-    for kind in (KIND_O, KIND_B, KIND_A):
-        for direction in DIRS:
-            ring_sum(kind, direction, 3, 1 - early(direction))
     pair(1)
+    across(3)
+    across(-3)
+    sum_on(split, 3, True)
+    compute(0)
     pair(-1)
-    compute(0)
+    sum_on(whole, 2, False)
+    sum_on(split, 3, False)
+    pair(0)
+    sum_on(whole, 1, True)
     across(2)
     across(-2)
-    for first in (True, False):
-        for kind in (KIND_O, KIND_B, KIND_A):
-            for direction in DIRS:
-                h = early(direction) if first else 1 - early(direction)
-                ring_sum(kind, direction, 2, h)
-    pair(0)
+    sum_on(split, 2, True)
+    sum_on(whole, 1, False)
+    sum_on(split, 2, False)
     across(1)
     across(-1)
-    for first in (True, False):
-        for kind in (KIND_O, KIND_B, KIND_A):
-            for direction in DIRS:
-                h = early(direction) if first else 1 - early(direction)
-                ring_sum(kind, direction, 1, h)
+    sum_on(split, 1, True)
+    sum_on(split, 1, False)
 
     load_moment.wait()
     total = xsum_buf[...]
+    if n_y > 1:
+        arrive(("y",), y_recv)
     for k in range(n_y - 1):
-        arrive(("y", k), y_recv.at[k])
         total = total + y_recv[k]
     drift_mean = total / (n_x * n_y)
     new_moment = outer_momentum * moment_buf[chosen] + drift_mean
-    moment_out[...] = new_moment
-    global_out[...] = global_buf[chosen] - outer_rate * (
+    new_global = global_buf[chosen] - outer_rate * (
         drift_mean + outer_momentum * new_moment
     )
+    for j in range(width // 128):
+        lane = slice(j * 128, (j + 1) * 128)
+        moment_out[j : j + 1, :] = new_moment[:, lane]
+        global_out[j : j + 1, :] = new_global[:, lane]
 
     across(0)
 
@@ -478,7 +478,7 @@
 
     for h in (0, 1):
         last_send[h] = last_sum(KIND_O, h).astype(jnp.bfloat16)
-        send(("last", h), last_send.at[h], last_recv.at[h], to_side)
+        send(LAST, ("last", h), last_send.at[h], last_recv.at[h], to_side)
     for h in (0, 1):
         grad_out[pl.ds(h * quarter, quarter), :] = last_sum(KIND_A, h)
     for h in (0, 1):
@@ -487,8 +487,17 @@
         grad_out[pl.ds(half + h * quarter, quarter), :] = total + last_recv[h].astype(
             jnp.float32
         )
-    for copy in started:
-        copy.wait_send()
+    drain(RING, gathered.at[pl.ds(0, 21 * half), :])
+    drain(SIDE, gathered.at[pl.ds(0, 9 * half), :])
+    drain(CORE, gathered.at[pl.ds(0, 16 * rows), :])
+    drain(CHIP, chip_send)
+    drain(PAIR, pair_send)
+    drain(SUM, ring_send.at[pl.ds(0, 42)])
+    drain(LAST, last_send)
+    if n_x > 1:
+        drain(ACROSS_X, x_recv)
+    if n_y > 1:
+        drain(ACROSS_Y, y_recv)
 
 
 def exchange(n_replica, inputs, doc_ids, values, cotangent, weights, local, current, moment, index):
@@ -501,17 +510,17 @@
     bf16, f32 = jnp.bfloat16, jnp.float32
     anywhere = pl.BlockSpec(memory_space=pl.ANY)
     vmem = pl.BlockSpec(memory_space=pltpu.VMEM)
-    n_sem = 192
     return pl.pallas_call(
         functools.partial(kernel, n_x, n_y, Lanes()),
         out_shape=(
             jax.ShapeDtypeStruct((rows, 2 * head), f32),
-            jax.ShapeDtypeStruct((1, width), f32),
-            jax.ShapeDtypeStruct((1, width), f32),
+            jax.ShapeDtypeStruct((width // 128, 128), f32),
+            jax.ShapeDtypeStruct((width // 128, 128), f32),
         ),
-        in_specs=[pl.BlockSpec(memory_space=pltpu.SMEM)] + [anywhere] * 8,
+        in_specs=[anywhere] * 9,
         out_specs=(vmem, vmem, vmem),
         scratch_shapes=[
+            pltpu.SMEM((1,), jnp.int32),
             pltpu.VMEM((tokens, width), bf16),
             pltpu.VMEM((width, tokens), bf16),
             pltpu.VMEM((rows, 2 * head), f32),
@@ -539,9 +548,9 @@
             pltpu.VMEM((48, quarter, 2 * head), bf16),
             pltpu.VMEM((2, quarter, 2 * head), bf16),
             pltpu.VMEM((2, quarter, 2 * head), bf16),
-            pltpu.SemaphoreType.DMA((8,)),
-            pltpu.SemaphoreType.DMA((n_sem,)),
-            pltpu.SemaphoreType.DMA((n_sem,)),
+            pltpu.SemaphoreType.DMA((9,)),
+            pltpu.SemaphoreType.DMA((9,)),
+            pltpu.SemaphoreType.DMA((98,)),
         ],
         compiler_params=pltpu.CompilerParams(
             collective_id=0, has_side_effects=True, vmem_limit_bytes=56 * 1024 * 1024
@@ -582,7 +591,14 @@
     weight_new = weights - learn_rate * (
         first_hat / (jnp.sqrt(second_hat) + 1e-08) + decay_rate * weights
     )
-    return (weight_new, first_new, second_new, new_global, new_moment)
+    shape = (1, inputs.shape[1])
+    return (
+        weight_new,
+        first_new,
+        second_new,
+        new_global.reshape(shape),
+        new_moment.reshape(shape),
+    )
 
 
 def solution(mesh):

time: 67.9 us -> 63 us (0.928)
  Pallas kernels: 61.7 us -> 56.8 us
    pallas_call x1, Pallas kernels: 61.7 us -> 56.8 us  [exchange(): pl.pallas_call(functools.partial(kernel, n_x, n_y, Lanes()), out_shape=(j...]
where the time goes in v2:
time: 63 us; the launch traced here: 62.7 us
  Pallas kernels  56.8 us (90%)
  local copies, waits for them, and re-layouts  2.7 us (4%)
  other arithmetic  1.82 us (3%)
  between operations  1.4 us (2%)
    pallas_call x1, Pallas kernels, exchange(): pl.pallas_call(functools.partial(kernel, n_x, n_y, Lanes()), out_shape=(j...  56.8 us
    unnamed x8, local copies, waits for them, and re-layouts  2.7 us
    sub x1, other arithmetic, on_device(): weights - learn_rate * (first_hat / (jnp.sqrt(second_hat) + 1e-08) + deca...  1.82 us

profile of v2, /device:TPU:6, one launch (start us, length us, event | category | flops | bytes accessed | tf_op | source)
XLA Modules:
  0.0 62.7 jit_solution(7602591150933359733)
XLA Ops:
  0.6 0.0 copy-start
  0.6 0.0 copy-start.2
  0.7 0.0 copy-start.1
  1.4 56.8 %shard_map.146 = (f32[192,256]{1,0:T(8,128)}, f32[48,128]{1,0:T(8,128)}, f32[48,128]{1,0:T(8,128)}) custom-call(s32[1]{0:T(128)S(6)} %copy.18.index_hbm, bf16[256,6144]{1,0:T(8,128)(2,1)} %x_hbm.1, s32[1,256]{1,0:T(1,128)} %doc_hbm.1, bf16[256,128]{1,0:T(8,128)(2,1)} %val_hbm.1, bf16[256,128]{1,0:T(8,128)(2,1)} %cot_hbm.1, f32[192,256]{1,0:T(8,128)} %w_hbm.1, ...), custom_call_target="tpu_custom_call" | custom-call | tf_op jit(solution)/shard_map/pallas_call | solution.py:513
  58.2 0.0 copy-done
  58.2 0.0 copy-done.2
  58.2 0.0 copy-done.1
  58.2 1.8 %multiply_subtract_fusion = (f32[192,256]{1,0:T(8,128)}, f32[192,256]{1,0:T(8,128)}, f32[192,256]{1,0:T(8,128)}) fusion(f32[192,256]{1,0:T(8,128)S(1)} %copy-done, f32[192,256]{1,0:T(8,128)} %get-tuple-element.8, f32[192,256]{1,0:T(8,128)S(1)} %copy-done.1, f32[192,256]{1,0:T(8,128)S(1)} %copy-done.2), kind=kLoop, calls=%fused_computation.2 | loop fusion | flops 737280 | bytes 1376256 | tf_op jit(solution)/shard_map/sub | solution.py:591
  60.0 1.3 %copy.19 = f32[1,6144]{1,0:T(1,128)} copy(f32[1,6144]{1,0:T(1,128)} %bitcast.5) | data formatting | bytes 49152
  61.4 1.3 %copy.20 = f32[1,6144]{1,0:T(1,128)} copy(f32[1,6144]{1,0:T(1,128)} %bitcast.4) | data formatting | bytes 49152
Async XLA Ops:
  0.6 57.5 %copy-start = (f32[192,256]{1,0:T(8,128)S(1)}, f32[192,256]{1,0:T(8,128)}, u32[]{:S(2)}) copy-start(f32[192,256]{1,0:T(8,128)} %w_hbm.1) | copy-start | bytes 589828
  0.6 57.5 %copy-start.2 = (f32[192,256]{1,0:T(8,128)S(1)}, f32[192,256]{1,0:T(8,128)}, u32[]{:S(2)}) copy-start(f32[192,256]{1,0:T(8,128)} %param.17) | copy-start | bytes 589828
  0.7 57.5 %copy-start.1 = (f32[192,256]{1,0:T(8,128)S(1)}, f32[192,256]{1,0:T(8,128)}, u32[]{:S(2)}) copy-start(f32[192,256]{1,0:T(8,128)} %param.16) | copy-start | bytes 589828

commit v3 on v2

--- a/solution.py
+++ b/solution.py
@@ -80,6 +80,7 @@
     load_sem,
     send_sem,
     recv_sem,
+    ready_sem,
 ):
     tokens, width = x_buf.shape
     head = val_buf.shape[1]
@@ -124,11 +125,35 @@
         describe(stream, ("core", 0), src, src, to_core).wait_send()
 
     barrier = pltpu.get_barrier_semaphore()
-    partners = [to_core, to_side, to_z[1], to_z[-1]] + to_x + to_y
-    for partner in partners:
+
+    def signal(sem, target):
         pl.semaphore_signal(
-            barrier, inc=1, device_id=partner, device_id_type=pl.DeviceIdType.MESH
+            sem, inc=1, device_id=target, device_id_type=pl.DeviceIdType.MESH
         )
+
+    near = [(other, z), (side, at_z(1)), (side, at_z(-1))]
+    far = [
+        {"replica": target["replica"], "shard": unit(side, z, 1)} for target in to_x + to_y
+    ]
+    for col, zz in near:
+        signal(barrier, {"shard": unit(col, zz, 0)})
+
+    @pl.when(core == 1)
+    def _():
+        signal(barrier, to_core)
+
+    for target in far:
+        signal(barrier, target)
+
+    def meet(count, counter, sem):
+        @pl.when(core == counter)
+        def _():
+            pl.semaphore_wait(barrier, count)
+            signal(sem, to_core)
+
+        @pl.when(core != counter)
+        def _():
+            pl.semaphore_wait(sem, 1)
 
     def load(n, src, dst):
         copy = pltpu.make_async_copy(src, dst, load_sem.at[n])
@@ -162,7 +187,7 @@
     local_copy = jnp.sum(jnp.where(picked, local_rows, 0.0), axis=0, keepdims=True)
     drift_buf[...] = (current - local_copy).astype(jnp.bfloat16).astype(jnp.float32)
 
-    pl.semaphore_wait(barrier, len(partners))
+    meet(2 * len(near) + 1, 0, ready_sem.at[0])
 
     def piece(kind, direction, d, cc):
         zz = at_z(-direction * d)
@@ -204,8 +229,6 @@
         ring_on(KIND_B, direction, 0)
     side_on(0, first_a)
     core_on(0, span(side, z, core, 0, rows))
-    for k, target in enumerate(to_x):
-        send(ACROSS_X, ("x",), drift_buf, x_recv.at[k], target)
 
     load_x.wait()
     block = 2 * rows
@@ -293,24 +316,25 @@
                 side_on(d, got)
             core_on(d, got)
 
-    fill(2)
+    arrive(("sideB",), their_b)
+    for direction in DIRS:
+        ring_on(KIND_O, direction, 0)
+    core_on(0, their_b)
+    fill(4)
     for d in range(1, 5):
         from_ring(KIND_A, d)
+        fill(2)
+        from_side(d - 1)
         from_ring(KIND_B, d)
-        if d == 1:
-            arrive(("sideB",), their_b)
-            for direction in DIRS:
-                ring_on(KIND_O, direction, 0)
-            core_on(0, their_b)
-        else:
-            from_ring(KIND_O, d - 1)
-        fill(3)
-        from_side(d - 1)
-        fill(3)
+        fill(2)
+        from_ring(KIND_O, d)
+        if d == 2 and far:
+            meet(2 * len(far), 1, ready_sem.at[1])
+            for k, target in enumerate(to_x):
+                send(ACROSS_X, ("x",), drift_buf, x_recv.at[k], target)
+        fill(2)
         queue_products(d - 1)
-    sums_over_x()
     from_side(4)
-    from_ring(KIND_O, 4)
     queue_products(4)
     fill(len(fillers))
 
@@ -411,6 +435,7 @@
     whole, split = (KIND_O, KIND_B), (KIND_A,)
     compute(4)
     compute(3)
+    sums_over_x()
     pair(4)
     sum_on(whole, 4, False)
     compute(-3)
@@ -421,28 +446,28 @@
     sum_on(whole, 3, True, (-1,))
     compute(-2)
     pair(2)
-    sum_on(whole, 3, False)
     compute(1)
     pair(-2)
     across(4)
     sum_on(split, 4, False)
-    sum_on(whole, 2, True)
+    sum_on(whole, 3, False)
     compute(-1)
     pair(1)
+    sum_on(whole, 2, True)
+    compute(0)
+    pair(-1)
     across(3)
     across(-3)
     sum_on(split, 3, True)
-    compute(0)
-    pair(-1)
-    sum_on(whole, 2, False)
     sum_on(split, 3, False)
     pair(0)
+    sum_on(whole, 2, False)
     sum_on(whole, 1, True)
     across(2)
     across(-2)
     sum_on(split, 2, True)
+    sum_on(split, 2, False)
     sum_on(whole, 1, False)
-    sum_on(split, 2, False)
     across(1)
     across(-1)
     sum_on(split, 1, True)
@@ -459,10 +484,8 @@
     new_global = global_buf[chosen] - outer_rate * (
         drift_mean + outer_momentum * new_moment
     )
-    for j in range(width // 128):
-        lane = slice(j * 128, (j + 1) * 128)
-        moment_out[j : j + 1, :] = new_moment[:, lane]
-        global_out[j : j + 1, :] = new_global[:, lane]
+    moment_out[...] = new_moment
+    global_out[...] = new_global
 
     across(0)
 
@@ -514,10 +537,10 @@
         functools.partial(kernel, n_x, n_y, Lanes()),
         out_shape=(
             jax.ShapeDtypeStruct((rows, 2 * head), f32),
-            jax.ShapeDtypeStruct((width // 128, 128), f32),
-            jax.ShapeDtypeStruct((width // 128, 128), f32),
+            jax.ShapeDtypeStruct((1, width), f32),
+            jax.ShapeDtypeStruct((1, width), f32),
         ),
-        in_specs=[anywhere] * 9,
+        in_specs=[pl.BlockSpec(memory_space=pltpu.HBM)] + [anywhere] * 8,
         out_specs=(vmem, vmem, vmem),
         scratch_shapes=[
             pltpu.SMEM((1,), jnp.int32),
@@ -551,11 +574,29 @@
             pltpu.SemaphoreType.DMA((9,)),
             pltpu.SemaphoreType.DMA((9,)),
             pltpu.SemaphoreType.DMA((98,)),
+            pltpu.SemaphoreType.REGULAR((2,)),
         ],
         compiler_params=pltpu.CompilerParams(
             collective_id=0, has_side_effects=True, vmem_limit_bytes=56 * 1024 * 1024
         ),
     )(index, inputs, doc_ids, values, cotangent, weights, local, current, moment)
+
+
+def finish(
+    grad, weights, moment1, moment2, new_global, new_moment, out_w, out_1, out_2, out_g, out_m
+):
+    gradient, rows = grad[...], weights[...]
+    first_new = beta_one * moment1[...] + (1.0 - beta_one) * gradient
+    second_new = beta_two * moment2[...] + (1.0 - beta_two) * gradient * gradient
+    first_hat = first_new / (1.0 - beta_one**ADAM_STEP)
+    second_hat = second_new / (1.0 - beta_two**ADAM_STEP)
+    out_w[...] = rows - learn_rate * (
+        first_hat / (jnp.sqrt(second_hat) + 1e-08) + decay_rate * rows
+    )
+    out_1[...] = first_new
+    out_2[...] = second_new
+    out_g[...] = new_global[...]
+    out_m[...] = new_moment[...]
 
 
 def on_device(
@@ -584,21 +625,15 @@
         frag_moment,
         frag_index,
     )
-    first_new = beta_one * moment1 + (1.0 - beta_one) * gradient
-    second_new = beta_two * moment2 + (1.0 - beta_two) * gradient * gradient
-    first_hat = first_new / (1.0 - beta_one**ADAM_STEP)
-    second_hat = second_new / (1.0 - beta_two**ADAM_STEP)
-    weight_new = weights - learn_rate * (
-        first_hat / (jnp.sqrt(second_hat) + 1e-08) + decay_rate * weights
-    )
-    shape = (1, inputs.shape[1])
-    return (
-        weight_new,
-        first_new,
-        second_new,
-        new_global.reshape(shape),
-        new_moment.reshape(shape),
-    )
+    vmem = pl.BlockSpec(memory_space=pltpu.VMEM)
+    like = jax.ShapeDtypeStruct(weights.shape, jnp.float32)
+    row = jax.ShapeDtypeStruct(new_global.shape, jnp.float32)
+    return pl.pallas_call(
+        finish,
+        out_shape=(like, like, like, row, row),
+        in_specs=[vmem] * 6,
+        out_specs=(vmem,) * 5,
+    )(gradient, weights, moment1, moment2, new_global, new_moment)
 
 
 def solution(mesh):

time: 63 us -> 56.3 us (0.89)
  local copies, waits for them, and re-layouts: 2.7 us -> 0 us
  Pallas kernels: 56.8 us -> 54.8 us
  other arithmetic: 1.82 us -> 0 us
    pallas_call x1, Pallas kernels: 56.8 us -> 52.6 us  [exchange(): pl.pallas_call(functools.partial(kernel, n_x, n_y, Lanes()), out_shape=(j...]
    unnamed x8 -> x0, local copies, waits for them, and re-layouts: 2.7 us -> none
    pallas_call x0 -> x1, Pallas kernels: none -> 2.16 us  [on_device(): pl.pallas_call(finish, out_shape=(like, like, like, row, row), in_specs=[...]
    sub x1 -> x0, other arithmetic: 1.82 us -> none  [on_device(): weights - learn_rate * (first_hat / (jnp.sqrt(second_hat) + 1e-08) + deca...]
where the time goes in v3:
time: 56.3 us; the launch traced here: 56.1 us
  Pallas kernels  54.8 us (97%)
  between operations  1.29 us (2%)
    pallas_call x1, Pallas kernels, exchange(): pl.pallas_call(functools.partial(kernel, n_x, n_y, Lanes()), out_shape=(j...  52.6 us
    pallas_call x1, Pallas kernels, on_device(): pl.pallas_call(finish, out_shape=(like, like, like, row, row), in_specs=[...  2.16 us

profile of v3, /device:TPU:6, one launch (start us, length us, event | category | flops | bytes accessed | tf_op | source)
XLA Modules:
  0.0 56.1 jit_solution(15629339842891142371)
XLA Ops:
  1.3 52.6 %shard_map.146 = (f32[192,256]{1,0:T(8,128)}, f32[1,6144]{1,0:T(1,128)}, f32[1,6144]{1,0:T(1,128)}) custom-call(s32[1]{0:T(128)S(6)} %copy.16.index_hbm, bf16[256,6144]{1,0:T(8,128)(2,1)} %x_hbm.1, s32[1,256]{1,0:T(1,128)} %doc_hbm.1, bf16[256,128]{1,0:T(8,128)(2,1)} %val_hbm.1, bf16[256,128]{1,0:T(8,128)(2,1)} %cot_hbm.1, f32[192,256]{1,0:T(8,128)} %weights.1, ...), custom_call_target="tpu_custom_call" | custom-call | tf_op jit(solution)/shard_map/pallas_call | solution.py:536
  53.9 2.2 %shard_map.147 = (f32[192,256]{1,0:T(8,128)}, f32[192,256]{1,0:T(8,128)}, f32[192,256]{1,0:T(8,128)}, f32[1,6144]{1,0:T(1,128)}, f32[1,6144]{1,0:T(1,128)}) custom-call(f32[192,256]{1,0:T(8,128)} %get-tuple-element.8.grad, f32[192,256]{1,0:T(8,128)} %weights.1, f32[192,256]{1,0:T(8,128)} %moment1.1, f32[192,256]{1,0:T(8,128)} %moment2.1, ...), custom_call_target="tpu_custom_call" | custom-call | tf_op jit(solution)/shard_map/pallas_call | solution.py:631

commit v4 on v3

--- a/solution.py
+++ b/solution.py
@@ -19,7 +19,7 @@
 outer_rate = 0.7
 
 Z = 8
-DIRS = (1, -1)
+WAYS = ((1, 0), (-1, 1))
 KIND_A, KIND_B, KIND_O = 0, 1, 2
 RING, SIDE, CORE, CHIP, PAIR, SUM, LAST, ACROSS_X, ACROSS_Y = range(9)
 ORDER = (4, 3, -3, 2, -2, 1, -1, 0)
@@ -28,9 +28,13 @@
 class Lanes:
     def __init__(self):
         self.numbers = {}
-
-    def __call__(self, *key):
-        return self.numbers.setdefault(key, len(self.numbers))
+        self.count = 0
+
+    def __call__(self, *key, width=1):
+        if key not in self.numbers:
+            self.numbers[key] = self.count
+            self.count += width
+        return self.numbers[key]
 
 
 def kernel(
@@ -101,7 +105,12 @@
 
     to_core = {"shard": unit(side, z, 1 - core)}
     to_side = {"shard": unit(other, z, core)}
-    to_z = {d: {"shard": unit(side, at_z(d), core)} for d in DIRS}
+
+    def to_z(way):
+        return {"shard": unit(side, at_z(way[0]), core)}
+
+    bit = jnp.where(z == 0, 1, 0)
+    ways = ((1 - 2 * bit, bit), (2 * bit - 1, 1 - bit))
     to_x = [{"replica": lax.rem(my_x + k, n_x) * n_y + my_y} for k in range(1, n_x)]
     to_y = [{"replica": my_x * n_y + lax.rem(my_y + k, n_y)} for k in range(1, n_y)]
 
@@ -110,7 +119,7 @@
             src_ref=src,
             dst_ref=dst,
             send_sem=send_sem.at[stream],
-            recv_sem=recv_sem.at[lanes(*key)],
+            recv_sem=recv_sem.at[key if not isinstance(key, tuple) else lanes(*key)],
             device_id=target,
             device_id_type=pl.DeviceIdType.MESH,
         )
@@ -122,7 +131,7 @@
         describe(0, key, dst, dst, to_core).wait_recv()
 
     def drain(stream, src):
-        describe(stream, ("core", 0), src, src, to_core).wait_send()
+        describe(stream, ("mine", 0), src, src, to_core).wait_send()
 
     barrier = pltpu.get_barrier_semaphore()
 
@@ -163,7 +172,6 @@
     load_w = load(0, w_hbm, w_buf)
     load_local = load(1, local_hbm, local_buf)
     load_global = load(2, global_hbm, global_buf)
-    load_x = load(3, x_hbm, x_buf)
     load_doc = load(4, doc_hbm, doc_buf)
     load_val = load(5, val_hbm, val_buf)
     load_cot = load(6, cot_hbm, cot_buf)
@@ -177,61 +185,68 @@
     load_w.wait()
     span(side, z, core, 0, rows)[...] = w_buf[...].astype(jnp.bfloat16)
 
-    load_index.wait()
-    chosen = index_buf[0]
-    load_local.wait()
-    load_global.wait()
-    current = global_buf[chosen]
-    local_rows = local_buf[...].astype(jnp.float32)
-    picked = lax.broadcasted_iota(jnp.int32, local_rows.shape, 0) == chosen
-    local_copy = jnp.sum(jnp.where(picked, local_rows, 0.0), axis=0, keepdims=True)
-    drift_buf[...] = (current - local_copy).astype(jnp.bfloat16).astype(jnp.float32)
-
     meet(2 * len(near) + 1, 0, ready_sem.at[0])
 
-    def piece(kind, direction, d, cc):
-        zz = at_z(-direction * d)
+    def piece(kind, way, d, cc, h):
+        zz = at_z(-way[0] * d)
         col = other if kind == KIND_O else side
         lo = 0 if kind == KIND_A else half
+        if h is None:
+            return span(col, zz, cc, lo, half)
+        return span(col, zz, cc, lo + h * quarter, quarter)
+
+    def part(way, q):
+        return None if q is None else way[1] if q == 0 else 1 - way[1]
+
+    def side_piece(way, d, cc, col):
+        zz = at_z(-way[0] * d)
         if d == 4:
-            return span(col, zz, cc, lo + (0 if direction == 1 else quarter), quarter)
-        return span(col, zz, cc, lo, half)
-
-    def side_piece(direction, d, cc, col):
-        zz = at_z(-direction * d)
+            return span(col, zz, cc, part(way, 0) * quarter, quarter)
+        return span(col, zz, cc, 0, half)
+
+    def ring_lane(kind, way, d, q):
+        if kind == KIND_B:
+            return lanes("ring", kind, d, width=2) + way[1]
         if d == 4:
-            return span(col, zz, cc, 0 if direction == 1 else quarter, quarter)
-        return span(col, zz, cc, 0, half)
-
-    def ring_on(kind, direction, d):
-        if d < 4:
-            src = piece(kind, direction, d, core)
-            if d == 3:
-                zz = at_z(-direction * d)
-                col = other if kind == KIND_O else side
-                lo = 0 if kind == KIND_A else half
-                src = span(col, zz, core, lo + (0 if direction == 1 else quarter), quarter)
-            send(RING, ("ring", kind, direction, d + 1), src, src, to_z[direction])
+            return lanes("ring", kind, d, width=2) + way[1]
+        return lanes("ring", kind, d, width=4) + 2 * q + way[1]
+
+    def ring_on(kind, way, d, q):
+        if d == 3 and q is None:
+            q = 0
+        if d < 3 or (d == 3 and q == 0):
+            src = piece(kind, way, d, core, part(way, q))
+            send(RING, ring_lane(kind, way, d + 1, q), src, src, to_z(way))
 
     def side_on(d, got):
         send(SIDE, ("side", d), got, got, to_side)
 
-    def core_on(d, got):
-        send(CORE, ("core", d), got, got, to_core)
+    def core_on(name, d, got):
+        send(CORE, (name, d), got, got, to_core)
 
     first_a = span(side, z, core, 0, half)
-    first_b = span(side, z, core, half, half)
-    their_b = span(other, z, core, half, half)
-    for direction in DIRS:
-        ring_on(KIND_A, direction, 0)
-    send(SIDE, ("sideB",), first_b, first_b, to_side)
-    for direction in DIRS:
-        ring_on(KIND_B, direction, 0)
-    side_on(0, first_a)
-    core_on(0, span(side, z, core, 0, rows))
-
-    load_x.wait()
+    for h in (0, 1):
+        first_b = span(side, z, core, half + h * quarter, quarter)
+        send(SIDE, ("sideB", h), first_b, first_b, to_side)
+    for q in (0, 1):
+        for way in WAYS:
+            ring_on(KIND_A, way, 0, q)
+    for way in WAYS:
+        ring_on(KIND_B, way, 0, None)
+    load_x = load(3, x_hbm, x_buf)
+
     block = 2 * rows
+
+    def make_drift():
+        load_index.wait()
+        load_local.wait()
+        load_global.wait()
+        chosen = index_buf[0]
+        current = global_buf[chosen]
+        local_rows = local_buf[...].astype(jnp.float32)
+        picked = lax.broadcasted_iota(jnp.int32, local_rows.shape, 0) == chosen
+        local_copy = jnp.sum(jnp.where(picked, local_rows, 0.0), axis=0, keepdims=True)
+        drift_buf[...] = (current - local_copy).astype(jnp.bfloat16).astype(jnp.float32)
 
     def transpose_block(p):
         cols = slice(p * block, (p + 1) * block)
@@ -271,26 +286,26 @@
         else:
             proj[...] += term
 
-    def arrive_core(d):
-        count = 2 * rows if d in (0, 4) else 4 * rows
-        arrive(("core", d), gathered.at[pl.ds(0, count), :])
-
-    fillers = [functools.partial(transpose_block, p) for p in range(2 * Z)]
-    fillers += [make_allowed, make_grad_att]
+    def arrive_core(name, d):
+        count = rows if d in (0, 4) else 2 * rows
+        arrive((name, d), gathered.at[pl.ds(0, count), :])
+
+    fillers = [make_drift, make_allowed, make_grad_att, load_x.wait]
+    fillers += [functools.partial(transpose_block, p) for p in range(2 * Z)]
 
     def fill(count=1):
         for _ in range(min(count, len(fillers))):
             fillers.pop(0)()
 
-    def queue_products(d):
-        fillers.append(functools.partial(arrive_core, d))
-        for direction in DIRS if 0 < d < 4 else (1,):
-            for col in (side, other):
-                fillers.append(
-                    functools.partial(
-                        multiply, col, at_z(-direction * d), first=d == 0 and col is side
-                    )
+    def queue_products(name, d):
+        col = side if name == "mine" else other
+        fillers.append(functools.partial(arrive_core, name, d))
+        for step, _ in WAYS if 0 < d < 4 else WAYS[:1]:
+            fillers.append(
+                functools.partial(
+                    multiply, col, at_z(-step * d), first=d == 0 and name == "mine"
                 )
+            )
 
     def sums_over_x():
         total = drift_buf[...]
@@ -304,39 +319,54 @@
 
     def from_side(d):
         arrive(("side", d), gathered.at[pl.ds(0, half if d in (0, 4) else rows), :])
-        for direction in DIRS if d else (1,):
-            core_on(d, side_piece(direction, d, core, other))
-
-    def from_ring(kind, d):
-        for direction in DIRS:
-            got = piece(kind, direction, d, core)
-            arrive(("ring", kind, direction, d), got)
-            ring_on(kind, direction, d)
+        for way in WAYS if d else WAYS[:1]:
+            core_on("theirs", d, side_piece(way, d, core, other))
+
+    def from_ring(kind, d, q):
+        for way in ways:
+            got = piece(kind, way, d, core, part(way, 0 if d == 4 else q))
+            arrive(ring_lane(kind, way, d, q), got)
+            ring_on(kind, way, d, q)
             if kind == KIND_A:
                 side_on(d, got)
-            core_on(d, got)
-
-    arrive(("sideB",), their_b)
-    for direction in DIRS:
-        ring_on(KIND_O, direction, 0)
-    core_on(0, their_b)
-    fill(4)
+            core_on("theirs" if kind == KIND_O else "mine", d, got)
+
+    fill(3)
     for d in range(1, 5):
-        from_ring(KIND_A, d)
-        fill(2)
-        from_side(d - 1)
-        from_ring(KIND_B, d)
-        fill(2)
-        from_ring(KIND_O, d)
+        for h in (0, 1):
+            if d < 4 or h == 0:
+                from_ring(KIND_A, d, h)
+            if d == 1:
+                their_b = span(other, z, core, half + h * quarter, quarter)
+                arrive(("sideB", h), their_b)
+                for way in WAYS:
+                    ring_on(KIND_O, way, 0, h if way[1] == 0 else 1 - h)
+                core_on("theirs", 0, their_b)
+            else:
+                from_ring(KIND_O, d - 1, h)
+        if d == 1:
+            side_on(0, first_a)
+            core_on("mine", 0, span(side, z, core, 0, rows))
+            queue_products("mine", 0)
+        fill(3)
+        from_ring(KIND_B, d, None)
+        queue_products("mine", d)
         if d == 2 and far:
             meet(2 * len(far), 1, ready_sem.at[1])
             for k, target in enumerate(to_x):
                 send(ACROSS_X, ("x",), drift_buf, x_recv.at[k], target)
-        fill(2)
-        queue_products(d - 1)
+        if d >= 2:
+            from_side(d - 2)
+            queue_products("theirs", d - 2)
+        fill(5)
+    from_side(3)
+    queue_products("theirs", 3)
+    fill(len(fillers) - 3)
+    from_ring(KIND_O, 4, None)
     from_side(4)
-    queue_products(4)
+    queue_products("theirs", 4)
     fill(len(fillers))
+    sums_over_x()
 
     input_scale = 1.0 / math.sqrt(width)
     score_scale = 1.0 / math.sqrt(head)
@@ -407,73 +437,87 @@
         arrive(("pair", i), pair_recv.at[i])
         sums[i, 0, :half] += pair_recv[i].astype(jnp.float32)
 
-    def early(direction):
-        return 1 if direction == 1 else 0
-
-    def slot(direction, kind, d, h):
-        return ((0 if direction == 1 else 1) * 3 + kind) * 8 + (d - 1) * 2 + h
-
-    def ring_sum(kind, direction, d, h):
-        delta = 4 if d == 4 else direction * d
+    def slot(way, kind, d, late):
+        return way[1] * 24 + kind * 8 + (d - 1) * 2 + late
+
+    first_sum = lanes("sum", width=48)
+
+    def ring_sum(kind, way, d, late):
+        i = 0 if d == 4 else 1 + 2 * (3 - d) + way[1]
         k = 1 if kind == KIND_O else 0
+        h = way[1] if late else 1 - way[1]
         lo = (0 if kind == KIND_A else half) + h * quarter
-        total = sums[place(delta), k, lo : lo + quarter]
-        if d < 3 or (d == 3 and h != early(direction)):
-            n = slot(direction, kind, d + 1, h)
-            arrive(("sum", n), ring_recv.at[n])
+        total = sums[i, k, pl.ds(pl.multiple_of(lo, 8), quarter)]
+        if d < 3 or (d == 3 and late):
+            n = slot(way, kind, d + 1, late)
+            arrive(first_sum + n, ring_recv.at[n])
             total = total + ring_recv[n].astype(jnp.float32)
-        n = slot(direction, kind, d, h)
+        n = slot(way, kind, d, late)
         ring_send[n] = total.astype(jnp.bfloat16)
-        send(SUM, ("sum", n), ring_send.at[n], ring_recv.at[n], to_z[direction])
-
-    def sum_on(kinds, d, first, directions=DIRS):
+        send(SUM, first_sum + n, ring_send.at[n], ring_recv.at[n], to_z(way))
+
+    def sum_on(kinds, d, first, among=ways):
         for kind in kinds:
-            for direction in directions:
-                h = early(direction) if first else 1 - early(direction)
-                ring_sum(kind, direction, d, h)
+            for way in among:
+                ring_sum(kind, way, d, 0 if first else 1)
 
     whole, split = (KIND_O, KIND_B), (KIND_A,)
     compute(4)
     compute(3)
-    sums_over_x()
+    compute(-3)
     pair(4)
     sum_on(whole, 4, False)
-    compute(-3)
+    compute(2)
     pair(3)
-    sum_on(whole, 3, True, (1,))
-    compute(2)
+    sum_on(whole, 3, True, WAYS[:1])
+    compute(-2)
     pair(-3)
-    sum_on(whole, 3, True, (-1,))
-    compute(-2)
+    sum_on(whole, 3, True, WAYS[1:])
+    compute(1)
     pair(2)
-    compute(1)
+    compute(-1)
     pair(-2)
+    sum_on(whole, 3, False)
+    compute(0)
+    pair(1)
     across(4)
     sum_on(split, 4, False)
-    sum_on(whole, 3, False)
-    compute(-1)
-    pair(1)
     sum_on(whole, 2, True)
-    compute(0)
     pair(-1)
+    sum_on(whole, 2, False)
     across(3)
     across(-3)
+    pair(0)
+    sum_on(split, 3, False)
     sum_on(split, 3, True)
-    sum_on(split, 3, False)
-    pair(0)
-    sum_on(whole, 2, False)
     sum_on(whole, 1, True)
+    sum_on(whole, 1, False)
     across(2)
     across(-2)
+    sum_on(split, 2, False)
     sum_on(split, 2, True)
-    sum_on(split, 2, False)
-    sum_on(whole, 1, False)
     across(1)
     across(-1)
+
+    def last_sum(kind, h):
+        k = 1 if kind == KIND_O else 0
+        lo = (0 if kind == KIND_A else half) + h * quarter
+        total = sums[place(0), k, lo : lo + quarter]
+        for way in WAYS:
+            n = slot(way, kind, 1, 1 if h == way[1] else 0)
+            arrive(first_sum + n, ring_recv.at[n])
+            total = total + ring_recv[n].astype(jnp.float32)
+        return total
+
+    for h in (0, 1):
+        last_send[h] = last_sum(KIND_O, h).astype(jnp.bfloat16)
+        send(LAST, ("last", h), last_send.at[h], last_recv.at[h], to_side)
+    sum_on(split, 1, False)
     sum_on(split, 1, True)
-    sum_on(split, 1, False)
+    across(0)
 
     load_moment.wait()
+    chosen = index_buf[0]
     total = xsum_buf[...]
     if n_y > 1:
         arrive(("y",), y_recv)
@@ -487,21 +531,6 @@
     moment_out[...] = new_moment
     global_out[...] = new_global
 
-    across(0)
-
-    def last_sum(kind, h):
-        k = 1 if kind == KIND_O else 0
-        lo = (0 if kind == KIND_A else half) + h * quarter
-        total = sums[place(0), k, lo : lo + quarter]
-        for direction in DIRS:
-            n = slot(direction, kind, 1, h)
-            arrive(("sum", n), ring_recv.at[n])
-            total = total + ring_recv[n].astype(jnp.float32)
-        return total
-
-    for h in (0, 1):
-        last_send[h] = last_sum(KIND_O, h).astype(jnp.bfloat16)
-        send(LAST, ("last", h), last_send.at[h], last_recv.at[h], to_side)
     for h in (0, 1):
         grad_out[pl.ds(h * quarter, quarter), :] = last_sum(KIND_A, h)
     for h in (0, 1):
@@ -573,7 +602,7 @@
             pltpu.VMEM((2, quarter, 2 * head), bf16),
             pltpu.SemaphoreType.DMA((9,)),
             pltpu.SemaphoreType.DMA((9,)),
-            pltpu.SemaphoreType.DMA((98,)),
+            pltpu.SemaphoreType.DMA((124,)),
             pltpu.SemaphoreType.REGULAR((2,)),
         ],
         compiler_params=pltpu.CompilerParams(

time: 56.3 us -> 55 us (0.977)
  Pallas kernels: 54.8 us -> 53.3 us
    pallas_call x1, Pallas kernels: 52.6 us -> 51.1 us  [exchange(): pl.pallas_call(functools.partial(kernel, n_x, n_y, Lanes()), out_shape=(j...]
where the time goes in v4:
time: 55 us; the launch traced here: 54.5 us
  Pallas kernels  53.3 us (97%)
  between operations  1.29 us (2%)
    pallas_call x1, Pallas kernels, exchange(): pl.pallas_call(functools.partial(kernel, n_x, n_y, Lanes()), out_shape=(j...  51.1 us
    pallas_call x1, Pallas kernels, on_device(): pl.pallas_call(finish, out_shape=(like, like, like, row, row), in_specs=[...  2.16 us

profile of v4, /device:TPU:6, one launch (start us, length us, event | category | flops | bytes accessed | tf_op | source)
XLA Modules:
  0.0 54.5 jit_solution(7014950618516996805)
XLA Ops:
  1.3 51.1 %shard_map.146 = (f32[192,256]{1,0:T(8,128)}, f32[1,6144]{1,0:T(1,128)}, f32[1,6144]{1,0:T(1,128)}) custom-call(s32[1]{0:T(128)S(6)} %copy.16.index_hbm, bf16[256,6144]{1,0:T(8,128)(2,1)} %x_hbm.1, s32[1,256]{1,0:T(1,128)} %doc_hbm.1, bf16[256,128]{1,0:T(8,128)(2,1)} %val_hbm.1, bf16[256,128]{1,0:T(8,128)(2,1)} %cot_hbm.1, f32[192,256]{1,0:T(8,128)} %weights.1, ...), custom_call_target="tpu_custom_call" | custom-call | tf_op jit(solution)/shard_map/pallas_call | solution.py:565
  52.4 2.2 %shard_map.147 = (f32[192,256]{1,0:T(8,128)}, f32[192,256]{1,0:T(8,128)}, f32[192,256]{1,0:T(8,128)}, f32[1,6144]{1,0:T(1,128)}, f32[1,6144]{1,0:T(1,128)}) custom-call(f32[192,256]{1,0:T(8,128)} %get-tuple-element.8.grad, f32[192,256]{1,0:T(8,128)} %weights.1, f32[192,256]{1,0:T(8,128)} %moment1.1, f32[192,256]{1,0:T(8,128)} %moment2.1, ...), custom_call_target="tpu_custom_call" | custom-call | tf_op jit(solution)/shard_map/pallas_call | solution.py:660

commit v5 on v4

--- a/solution.py
+++ b/solution.py
@@ -133,6 +133,13 @@
     def drain(stream, src):
         describe(stream, ("mine", 0), src, src, to_core).wait_send()
 
+    def load(n, src, dst):
+        copy = pltpu.make_async_copy(src, dst, load_sem.at[n])
+        copy.start()
+        return copy
+
+    load_w = load(0, w_hbm, w_buf)
+
     barrier = pltpu.get_barrier_semaphore()
 
     def signal(sem, target):
@@ -164,12 +171,6 @@
         def _():
             pl.semaphore_wait(sem, 1)
 
-    def load(n, src, dst):
-        copy = pltpu.make_async_copy(src, dst, load_sem.at[n])
-        copy.start()
-        return copy
-
-    load_w = load(0, w_hbm, w_buf)
     load_local = load(1, local_hbm, local_buf)
     load_global = load(2, global_hbm, global_buf)
     load_doc = load(4, doc_hbm, doc_buf)
@@ -370,34 +371,37 @@
 
     input_scale = 1.0 / math.sqrt(width)
     score_scale = 1.0 / math.sqrt(head)
-    exact = lax.Precision.HIGHEST
+
+    def halves(value):
+        high = value.astype(jnp.bfloat16)
+        return high, (value - high.astype(jnp.float32)).astype(jnp.bfloat16)
+
+    def product(left, right, left_dim, right_dim):
+        dims = (((left_dim,), (right_dim,)), ((), ()))
+        terms = ((0, 0), (0, 1), (1, 0))
+        return sum(
+            lax.dot_general(
+                left[i], right[j], dims, preferred_element_type=jnp.float32
+            )
+            for i, j in terms
+        )
+
     scaled = proj[...] * input_scale
     queries, keys_part = scaled[:, :head], scaled[:, head:]
     q_rate = lax.rsqrt(jnp.mean(queries * queries, axis=1, keepdims=True) + epsilon)
     k_rate = lax.rsqrt(jnp.mean(keys_part * keys_part, axis=1, keepdims=True) + epsilon)
     q_unit, k_unit = queries * q_rate, keys_part * k_rate
-    scores = (
-        lax.dot_general(
-            q_unit,
-            k_unit,
-            (((1,), (1,)), ((), ())),
-            precision=exact,
-            preferred_element_type=jnp.float32,
-        )
-        * score_scale
-    )
+    q_parts, k_parts = halves(q_unit), halves(k_unit)
+    scores = product(q_parts, k_parts, 1, 1) * score_scale
     raised = jnp.where(allowed_buf[...] > 0.5, jnp.exp(scores), 0.0)
     attention = raised / jnp.sum(raised, axis=1, keepdims=True)
     weighted = attention * grad_att[...]
     grad_scores = (
         weighted - attention * jnp.sum(weighted, axis=1, keepdims=True)
     ) * score_scale
-    grad_qunit = jnp.dot(
-        grad_scores, k_unit, precision=exact, preferred_element_type=jnp.float32
-    )
-    grad_kunit = jnp.dot(
-        grad_scores.T, q_unit, precision=exact, preferred_element_type=jnp.float32
-    )
+    score_parts = halves(grad_scores)
+    grad_qunit = product(score_parts, k_parts, 1, 0)
+    grad_kunit = product(score_parts, q_parts, 0, 0)
     grad_query = q_rate * (
         grad_qunit - q_unit * jnp.mean(grad_qunit * q_unit, axis=1, keepdims=True)
     )
@@ -464,9 +468,9 @@
     whole, split = (KIND_O, KIND_B), (KIND_A,)
     compute(4)
     compute(3)
-    compute(-3)
     pair(4)
     sum_on(whole, 4, False)
+    compute(-3)
     compute(2)
     pair(3)
     sum_on(whole, 3, True, WAYS[:1])

time: 55 us -> 54.2 us (0.985)
  Pallas kernels: 53.3 us -> 52.7 us
where the time goes in v5:
time: 54.2 us; the launch traced here: 54 us
  Pallas kernels  52.7 us (97%)
  between operations  1.29 us (2%)
    pallas_call x1, Pallas kernels, exchange(): pl.pallas_call(functools.partial(kernel, n_x, n_y, Lanes()), out_shape=(j...  50.5 us
    pallas_call x1, Pallas kernels, on_device(): pl.pallas_call(finish, out_shape=(like, like, like, row, row), in_specs=[...  2.16 us

profile of v5, /device:TPU:6, one launch (start us, length us, event | category | flops | bytes accessed | tf_op | source)
XLA Modules:
  0.0 54.0 jit_solution(9530132679707665633)
XLA Ops:
  1.3 50.5 %shard_map.146 = (f32[192,256]{1,0:T(8,128)}, f32[1,6144]{1,0:T(1,128)}, f32[1,6144]{1,0:T(1,128)}) custom-call(s32[1]{0:T(128)S(6)} %copy.16.index_hbm, bf16[256,6144]{1,0:T(8,128)(2,1)} %x_hbm.1, s32[1,256]{1,0:T(1,128)} %doc_hbm.1, bf16[256,128]{1,0:T(8,128)(2,1)} %val_hbm.1, bf16[256,128]{1,0:T(8,128)(2,1)} %cot_hbm.1, f32[192,256]{1,0:T(8,128)} %weights.1, ...), custom_call_target="tpu_custom_call" | custom-call | tf_op jit(solution)/shard_map/pallas_call | solution.py:569
  51.8 2.2 %shard_map.147 = (f32[192,256]{1,0:T(8,128)}, f32[192,256]{1,0:T(8,128)}, f32[192,256]{1,0:T(8,128)}, f32[1,6144]{1,0:T(1,128)}, f32[1,6144]{1,0:T(1,128)}) custom-call(f32[192,256]{1,0:T(8,128)} %get-tuple-element.8.grad, f32[192,256]{1,0:T(8,128)} %weights.1, f32[192,256]{1,0:T(8,128)} %moment1.1, f32[192,256]{1,0:T(8,128)} %moment2.1, ...), custom_call_target="tpu_custom_call" | custom-call | tf_op jit(solution)/shard_map/pallas_call | solution.py:664

commit v6 on v5

--- a/solution.py
+++ b/solution.py
@@ -427,6 +427,23 @@
             sums[i, k] = term[:rows]
         send(CHIP, ("chip", i), chip_send.at[i], chip_recv.at[i], to_core)
 
+    def compute_first():
+        both = ((1, other), (0, side))
+        starts = [unit(col, at_z(4), 0) * rows for _, col in both]
+        for (k, _), start in zip(both, starts):
+            chip_send[0, k] = jnp.dot(
+                xt_buf[pl.ds(pl.multiple_of(start + rows, 64), rows), :],
+                gp_buf[...],
+                preferred_element_type=jnp.float32,
+            ).astype(jnp.bfloat16)
+        send(CHIP, ("chip", 0), chip_send.at[0], chip_recv.at[0], to_core)
+        for (k, _), start in zip(both, starts):
+            sums[0, k] = jnp.dot(
+                xt_buf[pl.ds(pl.multiple_of(start, 128), rows), :],
+                gp_buf[...],
+                preferred_element_type=jnp.float32,
+            )
+
     def pair(delta):
         i = place(delta)
         arrive(("chip", i), chip_recv.at[i])
@@ -466,7 +483,7 @@
                 ring_sum(kind, way, d, 0 if first else 1)
 
     whole, split = (KIND_O, KIND_B), (KIND_A,)
-    compute(4)
+    compute_first()
     compute(3)
     pair(4)
     sum_on(whole, 4, False)

time: 54.2 us -> 54.1 us (level)
  no operation moved by 1% of the time
where the time goes in v6:
time: 54.1 us; the launch traced here: 53.9 us
  Pallas kernels  52.6 us (97%)
  between operations  1.29 us (2%)
    pallas_call x1, Pallas kernels, exchange(): pl.pallas_call(functools.partial(kernel, n_x, n_y, Lanes()), out_shape=(j...  50.4 us
    pallas_call x1, Pallas kernels, on_device(): pl.pallas_call(finish, out_shape=(like, like, like, row, row), in_specs=[...  2.16 us

profile of v6, /device:TPU:6, one launch (start us, length us, event | category | flops | bytes accessed | tf_op | source)
XLA Modules:
  0.0 53.9 jit_solution(6918210608177950019)
XLA Ops:
  1.3 50.4 %shard_map.146 = (f32[192,256]{1,0:T(8,128)}, f32[1,6144]{1,0:T(1,128)}, f32[1,6144]{1,0:T(1,128)}) custom-call(s32[1]{0:T(128)S(6)} %copy.16.index_hbm, bf16[256,6144]{1,0:T(8,128)(2,1)} %x_hbm.1, s32[1,256]{1,0:T(1,128)} %doc_hbm.1, bf16[256,128]{1,0:T(8,128)(2,1)} %val_hbm.1, bf16[256,128]{1,0:T(8,128)(2,1)} %cot_hbm.1, f32[192,256]{1,0:T(8,128)} %weights.1, ...), custom_call_target="tpu_custom_call" | custom-call | tf_op jit(solution)/shard_map/pallas_call | solution.py:586
  51.7 2.2 %shard_map.147 = (f32[192,256]{1,0:T(8,128)}, f32[192,256]{1,0:T(8,128)}, f32[192,256]{1,0:T(8,128)}, f32[1,6144]{1,0:T(1,128)}, f32[1,6144]{1,0:T(1,128)}) custom-call(f32[192,256]{1,0:T(8,128)} %get-tuple-element.8.grad, f32[192,256]{1,0:T(8,128)} %weights.1, f32[192,256]{1,0:T(8,128)} %moment1.1, f32[192,256]{1,0:T(8,128)} %moment2.1, ...), custom_call_target="tpu_custom_call" | custom-call | tf_op jit(solution)/shard_map/pallas_call | solution.py:681
